TPU v7x, 128 devices: a whole 4x4x4 slice. The times are simulated.
128 devices in a mesh: row: 8 (over x, y_hi), col: 16 (over y_lo, z, core).
Axes of the slice: x: 4, y: 4 (y_hi: 2, y_lo: 2; y = y_hi * 2 + y_lo), z: 4, core: 2. Of those that a mesh axis runs over, the one named last changes fastest.
Arguments:
- front_trailing: float32 [16384, 16384], P('row', 'col'), may hold values from -6 to 6
- panel_columns: float32 [16384, 1024], P('row', 'col'), may hold values from -0.1875 to 0.1875
- panel_rows: float32 [1024, 16384], P('row', 'col'), may hold values from -6 to 6
- pivots: int32 [1024], replicated, may hold values from 0 to 1023, each once
- diag_inverse: float32 [1024, 1024], replicated, may hold values from -0.1875 to 0.1875
- test_matrix: float32 [16384, 512], P('col'), may hold values from -0.046875 to 0.046875
Outputs:
- schur: float32 [16384, 16384], P('row', 'col')
- off_samples: float32 [16384, 512], P(('row', 'col'))
- leaf_blocks: float32 [16384, 128], P(('row', 'col'))
- group_gram: float32 [8, 512, 512], P('row')
Inputs may be any that keep to these rules, and one draw needn't show every extreme that they name: pivots names each of 0 to 1023 once.
All inputs are finite; a program needn't handle non-finite values.
Results may differ from a plain program's by a relative error of at most 0.000084.
Values sent between devices are 32-bit elements; how exact they have to be, the bound alone decides.
A program may use at most 128 MiB of HBM per device.

v0:
```python
import jax
import jax.numpy as jnp
from jax import lax
from jax.sharding import PartitionSpec as P

LEAF = 128


def swapped(block, axis, apart):
    count = lax.axis_size(axis)
    route = []
    for low in range(count):
        high = low | 1 << apart
        if high != low and high < count:
            route += [(low, high), (high, low)]
    return lax.ppermute(block, axis, route)


def from_root(block, axis, source):
    block = jnp.where(lax.axis_index(axis) == source, block, jnp.zeros_like(block))
    return lax.psum(block, axis)


def product(left, right):
    return jnp.dot(left, right, precision=lax.Precision.HIGHEST, preferred_element_type=jnp.float32)


def inner_gram(samples_local):
    return lax.dot_general(
        samples_local,
        samples_local,
        (((0,), (0,)), ((), ())),
        precision=lax.Precision.HIGHEST,
        preferred_element_type=jnp.float32,
    )


def body(front_trailing, panel_columns, panel_rows, pivots, diag_inverse, test_matrix):
    row_count = lax.axis_size("row")
    col_count = lax.axis_size("col")
    row_index = lax.axis_index("row")
    col_index = lax.axis_index("col")
    height, width = front_trailing.shape
    upper_full = lax.all_gather(panel_rows, "row", axis=0, tiled=True)
    upper = jnp.take(upper_full, pivots, axis=0)
    lower = product(lax.all_gather(panel_columns, "col", axis=1, tiled=True), diag_inverse)
    update = product(lower, upper)
    schur = front_trailing - update
    global_rows = row_index * height + jnp.arange(height, dtype=jnp.int32)
    global_cols = col_index * width + jnp.arange(width, dtype=jnp.int32)
    same_leaf = global_rows[:, None] // LEAF == global_cols[None, :] // LEAF
    masked = jnp.where(same_leaf, jnp.zeros_like(schur), schur)
    per_device = height // col_count
    summed = lax.psum(product(masked, test_matrix), "col")
    own_samples = lax.dynamic_slice_in_dim(summed, col_index * per_device, per_device, 0)
    gram = inner_gram(summed)
    partner = swapped(gram, "row", 0)
    group_gram = ((gram + partner) / (2 * height))[None]
    ratio = col_count // row_count
    blocks_count = width // LEAF
    region_start = col_index % ratio * width
    region = lax.dynamic_slice_in_dim(schur, region_start, width, 0)
    candidates = jnp.diagonal(
        region.reshape(blocks_count, LEAF, blocks_count, LEAF), axis1=0, axis2=2
    )
    candidates = jnp.moveaxis(candidates, -1, 0)
    received = [from_root(candidates, "col", row_index * ratio + source) for source in range(ratio)]
    stacked = jnp.stack(received).reshape(ratio * blocks_count, LEAF, LEAF)
    first_row = col_index * per_device
    picked = lax.dynamic_slice_in_dim(stacked, first_row // LEAF, per_device // LEAF, 0)
    leaf_blocks = picked.reshape(per_device, LEAF)
    return (schur, own_samples, leaf_blocks, group_gram)


def solution(mesh):
    placed = (P("row", "col"), P("row", "col"), P("row", "col"), P(), P(), P("col", None))
    return jax.shard_map(
        body,
        mesh=mesh,
        in_specs=placed,
        out_specs=(
            P("row", "col"),
            P(("row", "col"), None),
            P(("row", "col"), None),
            P("row", None, None),
        ),
        check_vma=False,
    )
```

profile of v0, /device:TPU:0, one launch (start us, length us, event | category | flops | bytes accessed | tf_op | source)
XLA Modules:
  0.0 403.2 jit_solution(12109506079082405454)
XLA Ops:
  7.2 0.7 all-gather.5.cloned.1.call-update
  8.0 0.7 all-gather.3.cloned.1.call-update
  8.8 0.7 compare_and_fusion
  9.5 0.7 fusion.19
  10.2 74.2 %all-gather.5.cloned.1.call-done = f32[1024,1024]{1,0:T(8,128)} async-done(((f32[128,1024]{1,0:T(8,128)}), f32[1024,1024]{1,0:T(8,128)}) %all-gather.5.cloned.1.call-update) | async-done | bytes 4194320 | tf_op jit(solution)/shard_map/all_gather | solution.py:44
  84.4 8.5 %gather_fusion = f32[1024,1024]{1,0:T(8,128)} fusion(f32[1024,1024]{1,0:T(8,128)} %all-gather.5.cloned.1.call-done, s32[1024]{0:T(1024)S(1)} %fusion.19), kind=kCustom, calls=%fused_computation | custom fusion | bytes 8392704 | tf_op jit(solution)/shard_map/jit(_take)/gather | solution.py:45
  92.9 43.2 %all-gather.3.cloned.1.call-done = f32[2048,1024]{0,1:T(8,128)} async-done(((f32[2048,64]{0,1:T(8,128)}), f32[2048,1024]{0,1:T(8,128)}) %all-gather.3.cloned.1.call-update) | async-done | bytes 8388624 | tf_op jit(solution)/shard_map/all_gather | solution.py:46
  136.1 30.1 %fusion.22 = f32[2048,1024]{1,0:T(8,128)S(1)} fusion(f32[2048,1024]{0,1:T(8,128)} %all-gather.3.cloned.1.call-done, f32[1024,1024]{1,0:T(8,128)} %param.10), kind=kOutput, calls=%fused_computation.45 | convolution fusion | flops 25769803776 | bytes 20971520 | tf_op jit(solution)/shard_map/dot_general | solution.py:25
  166.2 29.4 %fusion.8 = f32[2048,1024]{1,0:T(8,128)S(1)} fusion(f32[2048,1024]{1,0:T(8,128)S(1)} %copy-done.3, f32[2048,1024]{1,0:T(8,128)S(1)} %fusion.22, f32[1024,1024]{1,0:T(8,128)S(1)} %copy-done.1, pred[1024]{0:T(1024)(128)(4,1)S(1)} %compare_and_fusion), kind=kOutput, calls=%fused_computation.12 | convolution fusion | flops 25772949504 | bytes 29361152 | tf_op jit(solution)/shard_map/dot_general | solution.py:25
  195.7 0.3 dynamic-slice_bitcast_fusion
  196.0 3.1 copy-done.2
  199.1 1.0 copy.12
  200.1 2.7 copy.14
  202.8 2.8 gather_fusion.1
  205.6 17.4 %fusion = f32[2048,512]{1,0:T(8,128)} fusion(f32[1024,512]{1,0:T(8,128)S(1)} %copy-done, f32[2048,1024]{1,0:T(8,128)} %copy-done.2, s32[1024]{0:T(1024)S(1)} %add_select_fusion.1, s32[2048]{0:T(1024)S(1)} %add_select_fusion), kind=kOutput, calls=%fused_computation.2 | convolution fusion | flops 12889096192 | bytes 14692352 | tf_op jit(solution)/shard_map/dot_general | solution.py:25
  222.9 1.1 select_bitcast_fusion.1
  224.0 134.5 %all-reduce.3.cloned.1.call-done = (f32[2048,512]{1,0:T(8,128)}, f32[1,8,128,128]{3,2,1,0:T(8,128)}, f32[1,8,128,128]{3,2,1,0:T(8,128)}) async-done(((f32[2048,512]{1,0:T(8,128)}, f32[1,8,128,128]{3,2,1,0:T(8,128)}, f32[1,8,128,128]{3,2,1,0:T(8,128)}), (f32[2048,512]{1,0:T(8,128)}, f32[1,8,128,128]{3,2,1,0:T(8,128)}, f32[1,8,128,128]{3,2,1,0:T(8,128)})) %all-reduce.3.cloned.1.call-update) | async-done | bytes 5242896 | tf_op jit(solution)/shard_map/psum | solution.py:54
  358.5 10.2 %fusion.23 = f32[512,512]{1,0:T(8,128)S(1)} fusion(f32[2048,512]{1,0:T(8,128)} %get-tuple-element.4), kind=kOutput, calls=%fused_computation.46 | convolution fusion | flops 6442450944 | bytes 5242880 | tf_op jit(solution)/shard_map/dot_general | solution.py:29
  368.7 2.8 collective-permute-start
  371.5 1.3 pad_maximum_fusion
  372.8 0.6 dynamic-slice_bitcast_fusion.1
  373.4 1.7 constant_dynamic-slice_fusion
  375.1 19.2 %collective-permute-done = f32[512,512]{1,0:T(8,128)} collective-permute-done((f32[512,512]{1,0:T(8,128)S(1)}, f32[512,512]{1,0:T(8,128)}, u32[]{:S(2)}, u32[]{:S(2)}) %collective-permute-start) | collective-permute-done | bytes 1048608 | tf_op jit(solution)/shard_map/ppermute | solution.py:16
  394.2 2.4 multiply_bitcast_fusion
  (14 shorter events, 0.2 us)
Async XLA Ops:
  7.2 198.4 %copy-start = (f32[1024,512]{1,0:T(8,128)S(1)}, f32[1024,512]{1,0:T(8,128)}, u32[]{:S(2)}) copy-start(f32[1024,512]{1,0:T(8,128)} %param.11) | copy-start | bytes 6291460
  7.2 77.2 %all-gather.5.cloned.1.call-start = ((), (), s32[]{:S(2)}) async-start(), calls=%async_computation.1 | async-start | bytes 4718592 | tf_op jit(solution)/shard_map/all_gather | solution.py:44
  7.9 128.2 %all-gather.3.cloned.1.call-start = ((), (), s32[]{:S(2)}) async-start(), calls=%async_computation | async-start | bytes 8912896 | tf_op jit(solution)/shard_map/all_gather | solution.py:46
  8.7 349.8 %all-reduce.3.cloned.1.call-start = ((), (), s32[]{:S(2)}) async-start(), calls=%async_computation.2 | async-start | bytes 10485760 | tf_op jit(solution)/shard_map/psum | solution.py:54
  136.1 30.1 %copy-start.1 = (f32[1024,1024]{1,0:T(8,128)S(1)}, f32[1024,1024]{1,0:T(8,128)}, u32[]{:S(2)}) copy-start(f32[1024,1024]{1,0:T(8,128)} %gather_fusion) | copy-start | bytes 12582916
  136.1 30.1 %copy-start.3 = (f32[2048,1024]{1,0:T(8,128)S(1)}, f32[2048,1024]{1,0:T(8,128)}, u32[]{:S(2)}) copy-start(f32[2048,1024]{1,0:T(8,128)} %param.6) | copy-start | bytes 25165828
  195.7 3.4 copy-start.2
  368.7 25.6 %collective-permute-start = (f32[512,512]{1,0:T(8,128)S(1)}, f32[512,512]{1,0:T(8,128)}, u32[]{:S(2)}, u32[]{:S(2)}) collective-permute-start(f32[512,512]{1,0:T(8,128)S(1)} %fusion.23), channel_id=1, source_target_pairs={{0,16},{16,0},{32,48},{48,32},{64,80},{80,64},{96,112},{112,96},{1... | collective-permute-start | bytes 3145736 | tf_op jit(solution)/shard_map/ppermute | solution.py:16
Sparse Core Ops, SparseCore 0:
  10.3 74.0 all-gather.4
  86.1 49.9 all-gather.2
  224.1 134.3 all-reduce.2
where the time goes:
time: 404 us; the launch traced here: 403 us
  waiting for transfers between devices  272 us (67%)
  matrix products  87 us (22%)
  local copies, waits for them, and re-layouts  20.7 us (5%)
  between operations  13.9 us (3%)
  other arithmetic  6.2 us (2%)
    psum x1, waiting for transfers between devices, body(): summed = lax.psum(product(masked, test_matrix), 'col')  134 us
    dot_general x3, matrix products, product(): jnp.dot(left, right, precision=lax.Precision.HIGHEST, preferred_element_t...  76.9 us
    all_gather x1, waiting for transfers between devices, body(): upper_full = lax.all_gather(panel_rows, 'row', axis=0, tiled=True)  74.2 us
    all_gather x1, waiting for transfers between devices, body(): lax.all_gather(panel_columns, 'col', axis=1, tiled=True)  43.2 us
    ppermute x1, waiting for transfers between devices, swapped(): return lax.ppermute(block, axis, route)  19.2 us
    dot_general x1, matrix products, inner_gram(): lax.dot_general(samples_local, samples_local, (((0,), (0,)), ((), ())), p...  10.2 us
    gather x1, local copies, waits for them, and re-layouts, body(): upper = jnp.take(upper_full, pivots, axis=0)  8.52 us
  transfers between devices with their start and end apart: 4, of which 4 were waited for; matrix products, arithmetic and copies ran while one was open for 3% of the time, Pallas kernels for 0%

commit v1 on v0

v1 whole, which is shorter than its diff:
```python
import jax
import jax.numpy as jnp
from jax import lax
from jax.sharding import PartitionSpec as P

LEAF = 128


def product(left, right):
    return jnp.dot(left, right, precision=lax.Precision.HIGH, preferred_element_type=jnp.float32)


def body(front_trailing, panel_columns, panel_rows, pivots, diag_inverse, test_matrix):
    col_count = lax.axis_size("col")
    row_count = lax.axis_size("row")
    row_index = lax.axis_index("row")
    col_index = lax.axis_index("col")
    height, width = front_trailing.shape
    upper_full = lax.all_gather(panel_rows, "row", axis=0, tiled=True)
    left = lax.all_gather(panel_columns, "col", axis=1, tiled=True)
    upper = jnp.take(upper_full, pivots, axis=0)
    weight = product(diag_inverse, upper)
    schur = front_trailing - product(left, weight)
    rows = row_index * height + jnp.arange(height, dtype=jnp.int32)
    cols = col_index * width + jnp.arange(width, dtype=jnp.int32)
    same_leaf = rows[:, None] // LEAF == cols[None, :] // LEAF
    masked = jnp.where(same_leaf, jnp.zeros_like(schur), schur)
    partial = product(masked, test_matrix)
    count = width // LEAF
    ratio = col_count // row_count
    leaves = height // LEAF
    kept = []
    for leaf in range(leaves):
        held = col_index == row_index * ratio + leaf // count
        block = schur[leaf * LEAF : (leaf + 1) * LEAF, (leaf % count) * LEAF : (leaf % count + 1) * LEAF]
        kept.append(jnp.where(held, block, jnp.zeros_like(block)))
    both = jnp.concatenate([partial, jnp.concatenate(kept, axis=0)], axis=1)
    own = lax.psum_scatter(both, "col", scatter_dimension=0, tiled=True)
    own_samples = own[:, : partial.shape[1]]
    leaf_blocks = own[:, partial.shape[1] :]
    gram = lax.dot_general(
        own_samples,
        own_samples,
        (((0,), (0,)), ((), ())),
        precision=lax.Precision.HIGH,
        preferred_element_type=jnp.float32,
    )
    gram = lax.psum(gram, "col")
    route = [(i, i ^ 1) for i in range(row_count)]
    gram = gram + lax.ppermute(gram, "row", route)
    group_gram = (gram / (2 * height))[None]
    return (schur, own_samples, leaf_blocks, group_gram)


def solution(mesh):
    placed = (P("row", "col"), P("row", "col"), P("row", "col"), P(), P(), P("col", None))
    return jax.shard_map(
        body,
        mesh=mesh,
        in_specs=placed,
        out_specs=(
            P("row", "col"),
            P(("row", "col"), None),
            P(("row", "col"), None),
            P("row", None, None),
        ),
        check_vma=False,
    )
```

time: 404 us -> 393 us (0.973)
  matrix products: 87 us -> 45.9 us
  waiting for transfers between devices: 272 us -> 296 us
  local copies, waits for them, and re-layouts: 20.7 us -> 28.6 us
    reduce_scatter x0 -> x1, waiting for transfers between devices: none -> 70.5 us  [body(): own = lax.psum_scatter(both, 'col', scatter_dimension=0, tiled=True)]
    dot_general x4, matrix products: 87 us -> 45.9 us  [the longest x3 43.3 us: product(): jnp.dot(left, right, precision=lax.Precision.HIGH, preferred_element_type...]
    all_gather x1, waiting for transfers between devices: 43.2 us -> 25.2 us  [body(): left = lax.all_gather(panel_columns, 'col', axis=1, tiled=True)]
    unnamed x10 -> x12, local copies, waits for them, and re-layouts: 4.41 us -> 20 us
    psum x1, waiting for transfers between devices: 134 us -> 119 us  [body(): gram = lax.psum(gram, 'col')]
    all_gather x1, waiting for transfers between devices: 74.2 us -> 66.5 us  [body(): upper_full = lax.all_gather(panel_rows, 'row', axis=0, tiled=True)]
    ppermute x1, waiting for transfers between devices: 19.2 us -> 13.1 us  [body(): gram = gram + lax.ppermute(gram, 'row', route)]
  transfers between devices with their start and end apart: 4 -> 5, of which waited for: 4 -> 5; matrix products, arithmetic and copies ran while one was open for 3% -> 12% of each run, Pallas kernels for 0% -> 0%
where the time goes in v1:
time: 393 us
  waiting for transfers between devices  296 us (75%)
  matrix products  45.9 us (12%)
  local copies, waits for them, and re-layouts  28.6 us (7%)
  between operations  14 us (4%)
  other arithmetic  5.64 us (1%)
    psum x1, waiting for transfers between devices, body(): gram = lax.psum(gram, 'col')  119 us
    reduce_scatter x1, waiting for transfers between devices, body(): own = lax.psum_scatter(both, 'col', scatter_dimension=0, tiled=True)  70.5 us
    all_gather x1, waiting for transfers between devices, body(): upper_full = lax.all_gather(panel_rows, 'row', axis=0, tiled=True)  66.5 us
    dot_general x3, matrix products, product(): jnp.dot(left, right, precision=lax.Precision.HIGH, preferred_element_type...  43.3 us
    all_gather x1, waiting for transfers between devices, body(): left = lax.all_gather(panel_columns, 'col', axis=1, tiled=True)  25.2 us
    unnamed x12, local copies, waits for them, and re-layouts  20 us
    ppermute x1, waiting for transfers between devices, body(): gram = gram + lax.ppermute(gram, 'row', route)  13.1 us
    gather x1, local copies, waits for them, and re-layouts, body(): upper = jnp.take(upper_full, pivots, axis=0)  8.63 us
  transfers between devices with their start and end apart: 5, of which 5 were waited for; matrix products, arithmetic and copies ran while one was open for 12% of the time, Pallas kernels for 0%

profile of v1, /device:TPU:0, one launch (start us, length us, event | category | flops | bytes accessed | tf_op | source)
XLA Modules:
  0.0 392.7 jit_solution(6487991175751841340)
XLA Ops:
  7.2 0.0 all-gather.3.cloned.1.call-start
  7.2 0.7 all-gather.3.cloned.1.call-update
  7.9 0.0 all-gather.5.cloned.1.call-start
  8.0 0.7 all-gather.5.cloned.1.call-update
  8.7 0.0 reduce-scatter.2.cloned.1.call-start
  8.7 9.1 %copy.10 = f32[2048,1024]{0,1:T(8,128)} copy(f32[2048,1024]{1,0:T(8,128)} %param.6) | data formatting | bytes 16777216 | tf_op args[0]
  17.9 66.5 %all-gather.3.cloned.1.call-done = f32[1024,1024]{1,0:T(8,128)} async-done(((f32[128,1024]{1,0:T(8,128)}), f32[1024,1024]{1,0:T(8,128)}) %all-gather.3.cloned.1.call-update) | async-done | bytes 4194320 | tf_op jit(solution)/shard_map/all_gather | solution.py:19
  84.4 8.6 %gather_fusion = f32[1024,1024]{1,0:T(8,128)} fusion(f32[1024,1024]{1,0:T(8,128)} %all-gather.3.cloned.1.call-done, s32[1024]{0:T(1024)S(1)} %fusion.32), kind=kCustom, calls=%fused_computation | custom fusion | bytes 8392704 | tf_op jit(solution)/shard_map/jit(_take)/gather | solution.py:21
  93.0 17.9 %fusion.5 = f32[1024,1024]{1,0:T(8,128)} fusion(f32[1024,1024]{1,0:T(8,128)} %param.10, f32[1024,1024]{1,0:T(8,128)} %gather_fusion, pred[1024]{0:T(1024)(128)(4,1)S(1)} %compare_and_fusion), kind=kOutput, calls=%fused_computation.8 | convolution fusion | flops 6443499520 | bytes 12583936 | tf_op jit(solution)/shard_map/dot_general | solution.py:10
  110.9 25.2 %all-gather.5.cloned.1.call-done = f32[2048,1024]{0,1:T(8,128)} async-done(((f32[2048,64]{0,1:T(8,128)}), f32[2048,1024]{0,1:T(8,128)}) %all-gather.5.cloned.1.call-update) | async-done | bytes 8388624 | tf_op jit(solution)/shard_map/all_gather | solution.py:20
  136.1 17.8 %bitcast_subtract_fusion = f32[2048,1024]{0,1:T(8,128)S(1)} fusion(f32[2048,1024]{0,1:T(8,128)} %copy.10, f32[1024,1024]{1,0:T(8,128)} %fusion.5, f32[2048,1024]{0,1:T(8,128)} %all-gather.5.cloned.1.call-done), kind=kOutput, calls=%fused_computation.1 | convolution fusion | flops 12886999040 | bytes 29360128 | tf_op jit(solution)/shard_map/dot_general | solution.py:10
  154.3 7.6 %fusion = f32[2048,512]{0,1:T(8,128)S(1)} fusion(f32[1024,512]{1,0:T(8,128)S(1)} %copy-done, f32[2048,1024]{0,1:T(8,128)S(1)} %bitcast_subtract_fusion, s32[2048]{0:T(1024)S(1)} %add_select_fusion, s32[1024]{0:T(1024)S(1)} %add_select_fusion.1), kind=kOutput, calls=%fused_computation.2 | convolution fusion | flops 6446645248 | bytes 14692352 | tf_op jit(solution)/shard_map/dot_general | solution.py:10
  161.9 3.0 pad_maximum_fusion
  164.9 0.0 reduce-scatter.2.cloned.1.call-update
  164.9 0.0 all-reduce.2.cloned.1.call-start
  165.0 70.5 %reduce-scatter.2.cloned.1.call-done = f32[128,640]{0,1:T(8,128)} async-done(((f32[2048,640]{0,1:T(8,128)}), f32[128,640]{0,1:T(8,128)}) %reduce-scatter.2.cloned.1.call-update) | async-done | bytes 327696 | tf_op jit(solution)/shard_map/reduce_scatter | solution.py:38
  235.5 2.6 fusion.35
  238.1 119.0 %all-reduce.2.cloned.1.call-done = f32[512,512]{1,0:T(8,128)} async-done(((f32[512,512]{1,0:T(8,128)}), f32[512,512]{1,0:T(8,128)}) %all-reduce.2.cloned.1.call-update) | async-done | bytes 1048592 | tf_op jit(solution)/shard_map/psum | solution.py:48
  357.1 2.7 collective-permute-start
  359.8 9.2 %copy.11 = f32[2048,1024]{1,0:T(8,128)} copy(f32[2048,1024]{0,1:T(8,128)} %copy-done.1) | data formatting | bytes 16777216
  369.1 0.8 copy.12
  369.9 0.7 copy.13
  370.6 13.1 %collective-permute-done = f32[512,512]{1,0:T(8,128)} collective-permute-done((f32[512,512]{1,0:T(8,128)}, f32[512,512]{1,0:T(8,128)}, u32[]{:S(2)}, u32[]{:S(2)}) %collective-permute-start) | collective-permute-done | bytes 1048608 | tf_op jit(solution)/shard_map/ppermute | solution.py:50
  383.7 2.4 multiply_bitcast_fusion
  (33 shorter events, 0.3 us)
Async XLA Ops:
  7.2 147.1 %copy-start = (f32[1024,512]{1,0:T(8,128)S(1)}, f32[1024,512]{1,0:T(8,128)}, u32[]{:S(2)}) copy-start(f32[1024,512]{1,0:T(8,128)} %param.11) | copy-start | bytes 6291460
  7.2 77.2 %all-gather.3.cloned.1.call-start = ((), (), s32[]{:S(2)}) async-start(), calls=%async_computation.1 | async-start | bytes 4718592 | tf_op jit(solution)/shard_map/all_gather | solution.py:19
  7.9 128.2 %all-gather.5.cloned.1.call-start = ((), (), s32[]{:S(2)}) async-start(), calls=%async_computation.2 | async-start | bytes 8912896 | tf_op jit(solution)/shard_map/all_gather | solution.py:20
  8.7 226.8 %reduce-scatter.2.cloned.1.call-start = ((), (), s32[]{:S(2)}) async-start(), calls=%async_computation.3 | async-start | bytes 5570560 | tf_op jit(solution)/shard_map/reduce_scatter | solution.py:38
  8.7 9.2 %copy-start.3 = (s32[1024]{0:T(1024)S(1)}, s32[1024]{0:T(1024)}, u32[]{:S(2)}) copy-start(s32[1024]{0:T(1024)} %param.9) | copy-start | bytes 12292
  154.0 7.9 %copy-start.1 = (f32[2048,1024]{0,1:T(8,128)}, f32[2048,1024]{0,1:T(8,128)S(1)}, u32[]{:S(2)}) copy-start(f32[2048,1024]{0,1:T(8,128)S(1)} %bitcast_subtract_fusion) | copy-start | bytes 25165828
  164.9 192.2 %all-reduce.2.cloned.1.call-start = ((), (), s32[]{:S(2)}) async-start(), calls=%async_computation.4 | async-start | bytes 2097152 | tf_op jit(solution)/shard_map/psum | solution.py:48
  238.1 131.0 %slice-start = ((f32[128,640]{0,1:T(8,128)}), f32[128,512]{0,1:T(8,128)S(1)}, s32[]{:S(2)}) async-start(f32[128,640]{0,1:T(8,128)} %reduce-scatter.2.cloned.1.call-done), calls=%async_computation.5 | async-start | bytes 524288 | tf_op jit(solution)/shard_map/slice | solution.py:39
  238.1 131.8 %slice-start.1 = ((f32[128,640]{0,1:T(8,128)}), f32[128,128]{0,1:T(8,128)S(1)}, s32[]{:S(2)}) async-start(f32[128,640]{0,1:T(8,128)} %reduce-scatter.2.cloned.1.call-done), calls=%async_computation.6 | async-start | bytes 131072 | tf_op jit(solution)/shard_map/slice | solution.py:40
  357.1 26.6 %copy-start.2 = (f32[512,512]{1,0:T(8,128)S(1)}, f32[512,512]{1,0:T(8,128)}, u32[]{:S(2)}) copy-start(f32[512,512]{1,0:T(8,128)} %all-reduce.2.cloned.1.call-done) | copy-start | bytes 3145732
  357.1 26.6 %collective-permute-start = (f32[512,512]{1,0:T(8,128)}, f32[512,512]{1,0:T(8,128)}, u32[]{:S(2)}, u32[]{:S(2)}) collective-permute-start(f32[512,512]{1,0:T(8,128)} %all-reduce.2.cloned.1.call-done), channel_id=1, source_target_pairs={{0,16},{16,0},{32,48},{48,32},{64,80},{80,64},{96,112},{112,96},{1... | collective-permute-start | bytes 3145736 | tf_op jit(solution)/shard_map/ppermute | solution.py:50
Sparse Core Ops, SparseCore 0:
  10.3 74.0 all-gather.2
  86.1 49.9 all-gather.4
  165.0 70.3 reduce-scatter.1
  238.4 118.7 all-reduce.1

commit v2 on v1

v2 whole, which is shorter than its diff:
```python
import functools

import jax
import jax.numpy as jnp
from jax import lax
from jax.experimental import pallas as pl
from jax.experimental.pallas import tpu as pltpu
from jax.sharding import PartitionSpec as P

LEAF = 128
F32 = jnp.float32
BF16 = jnp.bfloat16
MESH = pl.DeviceIdType.MESH
TILE = 256


def split(x):
    high = x.astype(BF16)
    return high, (x - high.astype(F32)).astype(BF16)


def dot(a, b):
    return jnp.dot(a, b, preferred_element_type=F32)


def dot_nt(a, b):
    return lax.dot_general(a, b, (((1,), (1,)), ((), ())), preferred_element_type=F32)


def dot_tn(a, b):
    return lax.dot_general(a, b, (((0,), (0,)), ((), ())), preferred_element_type=F32)


def at_least(x, k):
    return pl.multiple_of(x, k)


class Sends:
    def __init__(self, sems):
        self.sems, self.made = sems, []

    def start(self, src, dst, recv, device):
        copy = pltpu.make_async_remote_copy(
            src_ref=src, dst_ref=dst, send_sem=self.sems.at[len(self.made)], recv_sem=recv,
            device_id=device, device_id_type=MESH,
        )
        copy.start()
        self.made.append(copy)

    def finish(self):
        for copy in self.made:
            copy.wait_send()


def arrived(dst, recv, send, device):
    pltpu.make_async_remote_copy(
        src_ref=dst, dst_ref=dst, send_sem=send, recv_sem=recv, device_id=device, device_id_type=MESH
    ).wait_recv()


class Gather:
    def __init__(self, sends, recv, source, place, plus, minus, pair):
        self.sends, self.recv, self.source, self.place = sends, recv, source, place
        self.plus, self.minus, self.pair = plus, minus, pair

    def begin(self):
        for piece in range(2):
            self.sends.start(self.source(piece), self.place(0, 0, piece), self.recv.at[piece], self.pair)
        for piece in range(2):
            self.sends.start(self.source(piece), self.place(0, 0, piece), self.recv.at[2 + piece], self.plus)
            self.sends.start(self.source(piece), self.place(0, 0, piece), self.recv.at[4 + piece], self.minus)

    def where(self, slot):
        pair = 1 if slot in (0, 4, 5, 6) else 0
        return {0: 0, 1: -1, 2: 1, 3: 2, 4: -1, 5: 1, 6: 2}[slot], pair

    def wait(self, slot, piece):
        ring, pair = self.where(slot)
        arrived(self.place(ring, pair, piece), self.recv.at[2 * slot + piece], self.sends.sems.at[0], self.plus)

    def spread(self, piece):
        ref = self.place(0, 1, piece)
        self.sends.start(ref, ref, self.recv.at[8 + piece], self.plus)
        self.sends.start(ref, ref, self.recv.at[10 + piece], self.minus)

    def relay(self, pair, piece):
        slot = 6 if pair else 3
        if piece == 0:
            ref = self.place(-1, pair, 0)
            self.sends.start(ref, ref, self.recv.at[2 * slot], self.plus)
        else:
            ref = self.place(1, pair, 1)
            self.sends.start(ref, ref, self.recv.at[2 * slot + 1], self.minus)


def kernel(
    front_hbm, pt_hbm, u_hbm, piv_ref, diag_hbm, test_hbm,
    schur_hbm, off_hbm, leaf_hbm, gram_hbm,
    pt, ug, dhi, dlo, wacc, whi, wlo, uh, ul, fr, t32, thi, tlo, part,
    rc, rz2, rz, ry, gl, gc, ga, go, lb,
    send_sems, p_recv, core_recv, u_recv, rs_send, rc_recv, rz2_recv, rz_recv, ry_recv,
    g_recv, leaf_send, leaf_recv, local, front_sem, out_sem,
):
    row, col = lax.axis_index("row"), lax.axis_index("col")
    x, yh = row // 2, row % 2
    yl, z, core = col // 8, (col % 8) // 2, col % 2
    y = yh * 2 + yl

    def p_col(dz, dy):
        return ((yl + dy) % 2) * 8 + ((z + dz + 4) % 4) * 2 + core

    def u_row(dx, dy):
        return ((x + dx + 4) % 4) * 2 + (yh + dy) % 2

    def plane(q):
        yy, zz = (y + q // 4) % 4, (z + q % 4) % 4
        return yy, zz

    partner = (row, col + 1 - 2 * core)
    z_plus, z_minus = (row, p_col(1, 0)), (row, p_col(-1, 0))
    y_pair = (row, p_col(0, 1))
    x_plus, x_minus = (u_row(1, 0), col), (u_row(-1, 0), col)
    h_pair = (u_row(0, 1), col)

    own_p = at_least(col * 64, 64)
    own_u = at_least(row * 128, 128)
    loads = [
        (diag_hbm, wacc, 0),
        (u_hbm, ug.at[pl.ds(own_u, 128), :], 1),
        (test_hbm, t32, 2),
        (pt_hbm, pt.at[pl.ds(own_p, 64), :], 3),
    ]
    loads = [pltpu.make_async_copy(src, dst, local.at[i]) for src, dst, i in loads]
    for copy in loads:
        copy.start()

    barrier = pltpu.get_barrier_semaphore()
    peers = [x_plus, x_minus]
    for q in range(16):
        yy, zz = plane(q)
        base = (yy % 2) * 8 + zz * 2
        r = x * 2 + yy // 2
        if q:
            peers.append((r, base + core))
        peers.append((r, base + 1 - core))
    for peer in peers:
        pl.semaphore_signal(barrier, inc=1, device_id=peer, device_id_type=MESH)
    pl.semaphore_wait(barrier, len(peers))

    sends = Sends(send_sems)

    def p_place(dz, dy, piece):
        return pt.at[pl.ds(at_least(p_col(dz, dy) * 64, 64), 64), pl.ds(piece * 1024, 1024)]

    def p_other(dz, dy, piece):
        c = p_col(dz, dy) + 1 - 2 * core
        return pt.at[pl.ds(at_least(c * 64, 64), 64), pl.ds(piece * 1024, 1024)]

    def u_place(dx, dy, piece):
        return ug.at[pl.ds(at_least(u_row(dx, dy) * 128 + piece * 64, 64), 64), :]

    pg = Gather(sends, p_recv, lambda i: pt_hbm.at[:, pl.ds(i * 1024, 1024)], p_place, z_plus, z_minus, y_pair)
    us = Gather(sends, u_recv, lambda i: u_hbm.at[pl.ds(i * 64, 64), :], u_place, x_plus, x_minus, h_pair)
    pg.begin()
    us.begin()
    for piece in range(2):
        sends.start(pg.source(piece), p_place(0, 0, piece), core_recv.at[14 + piece], partner)

    def hand(slot, piece):
        ring, pair = pg.where(slot)
        ref = p_place(ring, pair, piece)
        sends.start(ref, ref, core_recv.at[2 * slot + piece], partner)

    def tile_of(i):
        half = i // 4
        j = i % 4
        off = 2 - j + 3 * (j // 2) - 2 * (j // 3)
        return ((yl + 1 - half) % 2) * 4 + (z + off) % 4

    def front_copy(i):
        rows = pl.ds(at_least(tile_of(i) * TILE, TILE), TILE)
        return pltpu.make_async_copy(front_hbm.at[rows, :], fr.at[rows, :], front_sem.at[i])

    for i in range(8):
        front_copy(i).start()

    def one_hot(i, _):
        rows = pl.ds(at_least(i * TILE, TILE), TILE)
        ids = lax.broadcasted_iota(jnp.int32, (TILE, 1024), 0) + i * TILE
        whi[rows, :] = jnp.where(ids == piv_ref[...], 1.0, 0.0).astype(BF16)
        return 0

    lax.fori_loop(0, 4, one_hot, 0)
    loads[0].wait()

    def permute(i, _):
        rows = pl.ds(at_least(i * TILE, TILE), TILE)
        high, low = split(wacc[rows, :])
        dhi[rows, :] = dot_nt(high, whi[...]).astype(BF16)
        dlo[rows, :] = dot_nt(low, whi[...]).astype(BF16)
        return 0

    lax.fori_loop(0, 4, permute, 0)
    for copy in loads[1:]:
        copy.wait()

    def split_test(i, _):
        rows = pl.ds(at_least(i * TILE, TILE), TILE)
        high, low = split(t32[rows, :])
        thi[rows, :] = high
        tlo[rows, :] = low
        return 0

    lax.fori_loop(0, 4, split_test, 0)

    def weight(dx, first=False, last=False):
        start = at_least(((x + dx + 4) % 4) * TILE, TILE)
        high, low = split(ug[pl.ds(start, TILE), :])
        uh[...] = high
        ul[...] = low

        def step(i, _):
            rows = pl.ds(at_least(i * TILE, TILE), TILE)
            dh, dl = dhi[rows, pl.ds(start, TILE)], dlo[rows, pl.ds(start, TILE)]
            total = dot(dh, uh[...]) + dot(dl, uh[...]) + dot(dh, ul[...])
            if not first:
                total = total + wacc[rows, :]
            if last:
                high, low = split(total)
                whi[rows, :] = high
                wlo[rows, :] = low
            else:
                wacc[rows, :] = total
            return 0

        lax.fori_loop(0, 4, step, 0)

    for piece in range(2):
        for slot in (1, 2):
            pg.wait(slot, piece)
        pg.relay(0, piece)
        for slot in (1, 2):
            us.wait(slot, piece)
        us.relay(0, piece)
        for slot in (1, 2):
            hand(slot, piece)
    for piece in range(2):
        pg.wait(0, piece)
        pg.spread(piece)
        hand(0, piece)
    for piece in range(2):
        us.wait(0, piece)
        us.spread(piece)
    weight(0, first=True)
    for piece in range(2):
        pg.wait(3, piece)
        hand(3, piece)
        us.wait(3, piece)
    for piece in range(2):
        for slot in (4, 5):
            pg.wait(slot, piece)
        pg.relay(1, piece)
        for slot in (4, 5):
            us.wait(slot, piece)
        us.relay(1, piece)
        for slot in (4, 5):
            hand(slot, piece)
    weight(-1)
    weight(1)
    for piece in range(2):
        pg.wait(6, piece)
        hand(6, piece)
    for piece in range(2):
        us.wait(6, piece)
    weight(2, last=True)
    for slot in range(8):
        ring, pair = (0, 0) if slot == 7 else pg.where(slot)
        for piece in range(2):
            arrived(p_other(ring, pair, piece), core_recv.at[2 * slot + piece], send_sems.at[0], partner)

    def my_rows(i):
        return pl.ds(at_least(tile_of(i) * TILE + core * 128, 128), 128)

    def its_rows(i):
        return pl.ds(at_least(tile_of(i) * TILE + 128 - core * 128, 128), 128)

    def to_partner(i):
        return pltpu.make_async_remote_copy(
            src_ref=part.at[its_rows(i), :], dst_ref=rc.at[i], send_sem=rs_send.at[i], recv_sem=rc_recv.at[i],
            device_id=partner, device_id_type=MESH,
        )

    def far(i, half, way):
        return pltpu.make_async_remote_copy(
            src_ref=part.at[my_rows(i), pl.ds(way * 256, 256)], dst_ref=rz2.at[way, half],
            send_sem=rs_send.at[8 + 2 * way + half], recv_sem=rz2_recv.at[2 * way + half],
            device_id=z_minus if way else z_plus, device_id_type=MESH,
        )

    def near(i, half, way):
        return pltpu.make_async_remote_copy(
            src_ref=part.at[my_rows(i), :], dst_ref=rz.at[way, half],
            send_sem=rs_send.at[12 + 2 * way + half], recv_sem=rz_recv.at[2 * way + half],
            device_id=z_minus if way else z_plus, device_id_type=MESH,
        )

    def across():
        return pltpu.make_async_remote_copy(
            src_ref=part.at[my_rows(3), :], dst_ref=ry, send_sem=rs_send.at[16], recv_sem=ry_recv.at[0],
            device_id=y_pair, device_id_type=MESH,
        )

    def handle(i):
        half = i // 4
        j = i % 4
        mine = my_rows(i)
        to_partner(i).wait_recv()
        part[mine, :] = part[mine, :] + rc[i]

        @pl.when(j == 0)
        def _():
            far(i, half, 0).start()
            far(i, half, 1).start()

        for way in range(2):
            @pl.when(j == 1 + way)
            def _():
                far(i, half, way).wait_recv()
                lanes = pl.ds(way * 256, 256)
                part[mine, lanes] = part[mine, lanes] + rz2[way, half]
                near(i, half, way).start()

    def gather_line(i, half):
        mine = my_rows(i)
        near(i, half, 0).wait_recv()
        near(i, half, 1).wait_recv()
        part[mine, :] = part[mine, :] + rz[0, half] + rz[1, half]

    def out_copy(i):
        rows = pl.ds(at_least(tile_of(i) * TILE, TILE), TILE)
        return pltpu.make_async_copy(fr.at[rows, :], schur_hbm.at[rows, :], out_sem.at[i])

    def tile(i, _):
        m = tile_of(i)
        rows = pl.ds(at_least(m * TILE, TILE), TILE)
        front_copy(i).wait()
        high, low = split(pt[:, rows].T)
        update = dot(high, whi[...]) + dot(low, whi[...]) + dot(high, wlo[...])
        s = fr[rows, :] - update
        fr[rows, :] = s
        out_copy(i).start()
        row_leaf = row * 16 + m * 2 + lax.broadcasted_iota(jnp.int32, (TILE, 1024), 0) // LEAF
        col_leaf = col * 8 + lax.broadcasted_iota(jnp.int32, (TILE, 1024), 1) // LEAF
        high, low = split(jnp.where(row_leaf == col_leaf, 0.0, s))

        @pl.when(i > 0)
        def _():
            handle(i - 1)

        @pl.when(i == 7)
        def _():
            gather_line(3, 0)
            across().start()

        part[rows, :] = dot(high, thi[...]) + dot(low, thi[...]) + dot(high, tlo[...])
        to_partner(i).start()
        return 0

    lax.fori_loop(0, 8, tile, 0)

    side = col % 2

    def leaf_block(k):
        return fr.at[pl.ds(at_least((side * 8 + k) * LEAF, LEAF), LEAF), pl.ds(k * LEAF, LEAF)]

    def leaf_copy(k):
        return pltpu.make_async_remote_copy(
            src_ref=leaf_block(k), dst_ref=lb, send_sem=leaf_send.at[k], recv_sem=leaf_recv.at[0],
            device_id=(row, side * 8 + k), device_id_type=MESH,
        )

    for k in range(8):
        @pl.when((col // 2 == row) & (side * 8 + k != col))
        def _():
            leaf_copy(k).start()

        @pl.when((col // 2 == row) & (side * 8 + k == col))
        def _():
            pltpu.make_async_copy(leaf_block(k), lb, local.at[4]).start()

    handle(7)
    gather_line(7, 1)
    across().wait_recv()
    mine = my_rows(7)
    samples = part[mine, :] + ry[...]
    part[mine, :] = samples
    off_copy = pltpu.make_async_copy(part.at[mine, :], off_hbm, local.at[5])
    off_copy.start()

    high, low = split(samples)
    gl[...] = dot_tn(high, high) + dot_tn(low, high) + dot_tn(high, low)
    half_rows = pl.ds(at_least(core * 256, 256), 256)
    other_rows = pl.ds(at_least(256 - core * 256, 256), 256)
    sends.start(gl.at[other_rows, :], gc, g_recv.at[0], partner)
    arrived(gc, g_recv.at[0], send_sems.at[0], partner)
    gl[half_rows, :] = gl[half_rows, :] + gc[...]

    def piece(q):
        yy, zz = plane(q)
        device = (x * 2 + yy // 2, (yy % 2) * 8 + zz * 2 + core)
        return pl.ds(at_least(core * 256 + (yy * 4 + zz) * 16, 16), 16), device

    for q in range(1, 16):
        rows, device = piece(q)
        sends.start(gl.at[rows, :], ga.at[q], g_recv.at[q], device)
    total = gl[piece(0)[0], :]
    for q in range(1, 16):
        arrived(ga.at[q], g_recv.at[q], send_sems.at[0], partner)
        total = total + ga[q]
    own_rows = piece(0)[0]
    go[own_rows, :] = total * (1.0 / 4096)
    for q in range(1, 16):
        sends.start(go.at[own_rows, :], go.at[own_rows, :], g_recv.at[15 + q], piece(q)[1])
    for q in range(1, 16):
        rows = piece((4 - q // 4) % 4 * 4 + (4 - q % 4) % 4)[0]
        arrived(go.at[rows, :], g_recv.at[15 + q], send_sems.at[0], partner)
    sends.start(go.at[half_rows, :], go.at[half_rows, :], g_recv.at[31], partner)
    arrived(go.at[other_rows, :], g_recv.at[31], send_sems.at[0], partner)
    gram_copy = pltpu.make_async_copy(go, gram_hbm, local.at[6])
    gram_copy.start()

    holder = row * 2 + col // 8

    @pl.when(holder != col)
    def _():
        leaf_copy(0).wait_recv()

    @pl.when(holder == col)
    def _():
        pltpu.make_async_copy(leaf_block(0), lb, local.at[4]).wait()

    leaf_out = pltpu.make_async_copy(lb, leaf_hbm, local.at[7])
    leaf_out.start()
    for k in range(8):
        @pl.when((col // 2 == row) & (side * 8 + k != col))
        def _():
            leaf_copy(k).wait_send()

    for i in range(8):
        out_copy(i).wait()
        to_partner(i).wait_send()
    for half in range(2):
        for way in range(2):
            far(4 * half, half, way).wait_send()
            near(4 * half + 1 + way, half, way).wait_send()
    across().wait_send()
    sends.finish()
    off_copy.wait()
    gram_copy.wait()
    leaf_out.wait()


def body(front_trailing, panel_columns, panel_rows, pivots, diag_inverse, test_matrix):
    any_space = pl.BlockSpec(memory_space=pl.ANY)
    vmem, dma = pltpu.VMEM, pltpu.SemaphoreType.DMA
    schur, off, leaf, gram = pl.pallas_call(
        kernel,
        out_shape=(
            jax.ShapeDtypeStruct((2048, 1024), F32),
            jax.ShapeDtypeStruct((128, 512), F32),
            jax.ShapeDtypeStruct((128, 128), F32),
            jax.ShapeDtypeStruct((512, 512), F32),
        ),
        in_specs=[any_space, any_space, any_space, pl.BlockSpec(memory_space=pltpu.VMEM), any_space, any_space],
        out_specs=(any_space,) * 4,
        scratch_shapes=[
            vmem((1024, 2048), F32),
            vmem((1024, 1024), F32),
            vmem((1024, 1024), BF16),
            vmem((1024, 1024), BF16),
            vmem((1024, 1024), F32),
            vmem((1024, 1024), BF16),
            vmem((1024, 1024), BF16),
            vmem((TILE, 1024), BF16),
            vmem((TILE, 1024), BF16),
            vmem((2048, 1024), F32),
            vmem((1024, 512), F32),
            vmem((1024, 512), BF16),
            vmem((1024, 512), BF16),
            vmem((2048, 512), F32),
            vmem((8, 128, 512), F32),
            vmem((2, 2, 128, 256), F32),
            vmem((2, 2, 128, 512), F32),
            vmem((128, 512), F32),
            vmem((512, 512), F32),
            vmem((256, 512), F32),
            vmem((16, 16, 512), F32),
            vmem((512, 512), F32),
            vmem((128, 128), F32),
            dma((80,)),
            dma((14,)),
            dma((16,)),
            dma((14,)),
            dma((17,)),
            dma((8,)),
            dma((4,)),
            dma((4,)),
            dma((1,)),
            dma((32,)),
            dma((8,)),
            dma((1,)),
            dma((8,)),
            dma((8,)),
            dma((8,)),
        ],
        compiler_params=pltpu.CompilerParams(
            collective_id=0, has_side_effects=True, vmem_limit_bytes=64_000_000
        ),
        name="front",
    )(front_trailing, panel_columns.T, panel_rows, pivots.reshape(1, -1), diag_inverse, test_matrix)
    return schur, off, leaf, gram[None]


def solution(mesh):
    placed = (P("row", "col"), P("row", "col"), P("row", "col"), P(), P(), P("col", None))
    return jax.shard_map(
        body,
        mesh=mesh,
        in_specs=placed,
        out_specs=(
            P("row", "col"),
            P(("row", "col"), None),
            P(("row", "col"), None),
            P("row", None, None),
        ),
        check_vma=False,
    )
```

time: 393 us -> 121 us (0.31)
  waiting for transfers between devices: 296 us -> 0 us
  Pallas kernels: 0 us -> 108 us
  matrix products: 45.9 us -> 0 us
  local copies, waits for them, and re-layouts: 28.6 us -> 10.9 us
  between operations: 14 us -> 0.67 us
  other arithmetic: 5.64 us -> 0 us
    psum x1 -> x0, waiting for transfers between devices: 119 us -> none  [body(): gram = lax.psum(gram, 'col')]
    pallas_call x0 -> x1, Pallas kernels: none -> 108 us  [body(): pl.pallas_call(kernel, out_shape=(jax.ShapeDtypeStruct((2048, 1024), F32)...]
    all_gather x2 -> x0, waiting for transfers between devices: 91.7 us -> none  [the longest x1 66.5 us: body(): upper_full = lax.all_gather(panel_rows, 'row', axis=0, tiled=True)]
    reduce_scatter x1 -> x0, waiting for transfers between devices: 70.5 us -> none  [body(): own = lax.psum_scatter(both, 'col', scatter_dimension=0, tiled=True)]
    dot_general x4 -> x0, matrix products: 45.9 us -> none  [the longest x3 43.3 us: product(): jnp.dot(left, right, precision=lax.Precision.HIGH, preferred_element_type...]
    ppermute x1 -> x0, waiting for transfers between devices: 13.1 us -> none  [body(): gram = gram + lax.ppermute(gram, 'row', route)]
    unnamed x12 -> x10, local copies, waits for them, and re-layouts: 20 us -> 10.9 us
    gather x1 -> x0, local copies, waits for them, and re-layouts: 8.63 us -> none  [body(): upper = jnp.take(upper_full, pivots, axis=0)]
  transfers between devices with their start and end apart: 5 -> 0, of which waited for: 5 -> 0; matrix products, arithmetic and copies ran while one was open for 12% -> 0% of each run, Pallas kernels for 0% -> 0%
where the time goes in v2:
time: 121 us; the launch traced here: 120 us
  Pallas kernels  108 us (89%)
  local copies, waits for them, and re-layouts  10.9 us (9%)
    pallas_call x1, Pallas kernels, body(): pl.pallas_call(kernel, out_shape=(jax.ShapeDtypeStruct((2048, 1024), F32)...  108 us
    unnamed x10, local copies, waits for them, and re-layouts  10.9 us

profile of v2, /device:TPU:0, one launch (start us, length us, event | category | flops | bytes accessed | tf_op | source)
XLA Modules:
  0.0 119.6 jit_solution(14258157482684325098)
XLA Ops:
  0.6 108.1 %front.1 = (f32[2048,1024]{1,0:T(8,128)}, f32[128,512]{1,0:T(8,128)}, f32[128,128]{1,0:T(8,128)}, f32[512,512]{1,0:T(8,128)}) custom-call(f32[2048,1024]{1,0:T(8,128)} %front_hbm.1, f32[64,2048]{1,0:T(8,128)} %bitcast.4, f32[128,1024]{1,0:T(8,128)} %u_hbm.1, s32[1,1024]{1,0:T(1,128)} %bitcast.5, f32[1024,1024]{1,0:T(8,128)} %diag_hbm.1, f32[1024,512]{1,0:T(8,128)} %test_hbm.1), custom_call_target="tpu_custom_call" | custom-call | tf_op jit(solution)/shard_map/front/pallas_call | solution.py:466
  108.7 0.0 copy-start.1
  108.7 0.0 copy-start.2
  108.8 0.0 copy-start
  108.8 8.5 %copy.14 = f32[2048,1024]{1,0:T(8,128)} copy(f32[2048,1024]{1,0:T(8,128)} %get-tuple-element.16) | data formatting | bytes 16777216
  117.3 0.0 copy-done.1
  117.3 0.7 copy.15
  118.0 0.0 copy-done.2
  118.0 0.6 copy.16
  118.7 0.0 copy-done
  118.7 1.0 copy.17
Async XLA Ops:
  108.7 8.6 %copy-start.1 = (f32[128,512]{1,0:T(8,128)S(1)}, f32[128,512]{1,0:T(8,128)}, u32[]{:S(2)}) copy-start(f32[128,512]{1,0:T(8,128)} %get-tuple-element.17) | copy-start | bytes 786436
  108.7 9.3 %copy-start.2 = (f32[128,128]{1,0:T(8,128)S(1)}, f32[128,128]{1,0:T(8,128)}, u32[]{:S(2)}) copy-start(f32[128,128]{1,0:T(8,128)} %get-tuple-element.18) | copy-start | bytes 196612
  108.8 9.9 %copy-start = (f32[512,512]{1,0:T(8,128)S(1)}, f32[512,512]{1,0:T(8,128)}, u32[]{:S(2)}) copy-start(f32[512,512]{1,0:T(8,128)} %get-tuple-element.11) | copy-start | bytes 3145732

commit v3 on v2

v3 whole, which is shorter than its diff:
```python
import functools

import jax
import jax.numpy as jnp
from jax import lax
from jax.experimental import pallas as pl
from jax.experimental.pallas import tpu as pltpu
from jax.sharding import PartitionSpec as P

LEAF = 128
F32 = jnp.float32
BF16 = jnp.bfloat16
MESH = pl.DeviceIdType.MESH
TILE = 256


def split(x):
    high = x.astype(BF16)
    return high, (x - high.astype(F32)).astype(BF16)


def dot(a, b):
    return jnp.dot(a, b, preferred_element_type=F32)


def dot_nt(a, b):
    return lax.dot_general(a, b, (((1,), (1,)), ((), ())), preferred_element_type=F32)


def dot_tn(a, b):
    return lax.dot_general(a, b, (((0,), (0,)), ((), ())), preferred_element_type=F32)


def at_least(x, k):
    return pl.multiple_of(x, k)


class Sends:
    def __init__(self, sems):
        self.sems, self.made = sems, []

    def start(self, src, dst, recv, device):
        copy = pltpu.make_async_remote_copy(
            src_ref=src, dst_ref=dst, send_sem=self.sems.at[len(self.made)], recv_sem=recv,
            device_id=device, device_id_type=MESH,
        )
        copy.start()
        self.made.append(copy)

    def finish(self):
        for copy in self.made:
            copy.wait_send()


def arrived(dst, recv, send, device):
    pltpu.make_async_remote_copy(
        src_ref=dst, dst_ref=dst, send_sem=send, recv_sem=recv, device_id=device, device_id_type=MESH
    ).wait_recv()


PIECES = 4


class Gather:
    def __init__(self, sends, recv, source, place, plus, minus, pair):
        self.sends, self.recv, self.source, self.place = sends, recv, source, place
        self.plus, self.minus, self.pair = plus, minus, pair

    def begin(self):
        for piece in range(PIECES):
            src, dst = self.source(piece), self.place(0, 0, piece)
            self.sends.start(src, dst, self.recv.at[piece], self.pair)
            self.sends.start(src, dst, self.recv.at[PIECES + piece], self.plus)
            self.sends.start(src, dst, self.recv.at[2 * PIECES + piece], self.minus)

    def where(self, slot):
        return {0: 0, 1: -1, 2: 1, 3: 2, 4: -1, 5: 1, 6: 2, 7: 0}[slot], int(slot in (0, 4, 5, 6))

    def wait(self, slot, *pieces):
        ring, pair = self.where(slot)
        for piece in pieces:
            arrived(
                self.place(ring, pair, piece), self.recv.at[PIECES * slot + piece], self.sends.sems.at[0], self.plus
            )

    def spread(self, *pieces):
        self.wait(0, *pieces)
        for piece in pieces:
            ref = self.place(0, 1, piece)
            self.sends.start(ref, ref, self.recv.at[4 * PIECES + piece], self.plus)
            self.sends.start(ref, ref, self.recv.at[5 * PIECES + piece], self.minus)

    def relay(self, pair, *pieces):
        slot = 6 if pair else 3
        for piece in pieces:
            ring, device = (-1, self.plus) if piece < 2 else (1, self.minus)
            self.wait((1 if ring < 0 else 2) + 3 * pair, piece)
            ref = self.place(ring, pair, piece)
            self.sends.start(ref, ref, self.recv.at[PIECES * slot + piece], device)


def kernel(
    front_hbm, pt_hbm, u_hbm, piv_ref, diag_hbm, test_hbm,
    schur, off, leaf, gram,
    pt, ug, dhi, dlo, wacc, whi, wlo, uh, ul, ph, pl_, fr, thi, tlo, part,
    rc, rz2, rz, ry, sx, gl, ga, gf,
    send_sems, p_recv, core_recv, u_recv, rs_send, rc_recv, rz2_recv, rz_recv, ry_recv,
    g_recv, leaf_send, leaf_recv, local, front_sem,
):
    row, col = lax.axis_index("row"), lax.axis_index("col")
    x, yh = row // 2, row % 2
    yl, z, core = col // 8, (col % 8) // 2, col % 2
    y = yh * 2 + yl

    def p_col(dz, dy):
        return ((yl + dy) % 2) * 8 + ((z + dz + 4) % 4) * 2 + core

    def u_row(dx, dy):
        return ((x + dx + 4) % 4) * 2 + (yh + dy) % 2

    def plane(q):
        yy, zz = (y + q // 4) % 4, (z + q % 4) % 4
        return yy, zz

    partner = (row, col + 1 - 2 * core)
    z_plus, z_minus = (row, p_col(1, 0)), (row, p_col(-1, 0))
    y_pair = (row, p_col(0, 1))
    x_plus, x_minus = (u_row(1, 0), col), (u_row(-1, 0), col)
    h_pair = (u_row(0, 1), col)

    own_p = at_least(col * 64, 64)
    own_u = at_least(yh * 512 + x * 128, 128)
    loads = [
        (diag_hbm, wacc, 0),
        (u_hbm, ug.at[pl.ds(own_u, 128), :], 1),
        (test_hbm, part.at[pl.ds(0, 1024), :], 2),
        (pt_hbm, pt.at[pl.ds(own_p, 64), :], 3),
    ]
    loads = [pltpu.make_async_copy(src, dst, local.at[i]) for src, dst, i in loads]
    for copy in loads:
        copy.start()

    barrier = pltpu.get_barrier_semaphore()
    peers = [x_plus, x_minus, h_pair, y_pair, z_plus, z_minus, partner]
    for peer in peers:
        pl.semaphore_signal(barrier, inc=1, device_id=peer, device_id_type=MESH)
    pl.semaphore_wait(barrier, len(peers))

    sends = Sends(send_sems)

    def p_place(dz, dy, piece):
        return pt.at[pl.ds(at_least(p_col(dz, dy) * 64, 64), 64), pl.ds(piece * 512, 512)]

    def p_other(dz, dy, piece):
        c = p_col(dz, dy) + 1 - 2 * core
        return pt.at[pl.ds(at_least(c * 64, 64), 64), pl.ds(piece * 512, 512)]

    def u_place(dx, dy, piece):
        return ug.at[pl.ds(at_least(((yh + dy) % 2) * 512 + ((x + dx + 4) % 4) * 128 + piece * 32, 32), 32), :]

    pg = Gather(sends, p_recv, lambda i: pt_hbm.at[:, pl.ds(i * 512, 512)], p_place, z_plus, z_minus, y_pair)
    us = Gather(sends, u_recv, lambda i: u_hbm.at[pl.ds(i * 32, 32), :], u_place, x_plus, x_minus, h_pair)
    pg.begin()
    us.begin()
    for piece in range(PIECES):
        sends.start(pg.source(piece), p_place(0, 0, piece), core_recv.at[7 * PIECES + piece], partner)

    def hand(slot, *pieces):
        ring, pair = pg.where(slot)
        for piece in pieces:
            ref = p_place(ring, pair, piece)
            sends.start(ref, ref, core_recv.at[PIECES * slot + piece], partner)

    def tile_of(i):
        half = i // 4
        j = i % 4
        off = 2 - j + 3 * (j // 2) - 2 * (j // 3)
        return ((yl + 1 - half) % 2) * 4 + (z + off) % 4

    def front_copy(i):
        rows = pl.ds(at_least(tile_of(i) * TILE, TILE), TILE)
        return pltpu.make_async_copy(front_hbm.at[rows, :], fr.at[i % 2], front_sem.at[i % 2])

    front_copy(0).start()

    def one_hot(i, _):
        rows = pl.ds(at_least(i * TILE, TILE), TILE)
        k = lax.broadcasted_iota(jnp.int32, (TILE, 1024), 0)
        ids = (i % 2) * 512 + (i // 2) * 128 + k + (k // 128) * 128
        whi[rows, :] = jnp.where(ids == piv_ref[...], 1.0, 0.0).astype(BF16)
        return 0

    lax.fori_loop(0, 4, one_hot, 0)
    loads[0].wait()

    def permute(i, _):
        rows = pl.ds(at_least(i * TILE, TILE), TILE)
        high, low = split(wacc[rows, :])
        dhi[rows, :] = dot_nt(high, whi[...]).astype(BF16)
        dlo[rows, :] = dot_nt(low, whi[...]).astype(BF16)
        return 0

    lax.fori_loop(0, 3, permute, 0)
    pg.relay(0, 0, 1, 2)
    us.relay(0, 0, 1, 2)
    lax.fori_loop(3, 4, permute, 0)
    pg.relay(0, 3)
    us.relay(0, 3)
    pg.spread(0)
    us.spread(0)
    for copy in loads[1:]:
        copy.wait()

    def split_test(i, _):
        rows = pl.ds(at_least(i * TILE, TILE), TILE)
        high, low = split(part[rows, :])
        thi[rows, :] = high
        tlo[rows, :] = low
        return 0

    lax.fori_loop(0, 4, split_test, 0)

    def weight(line, pair, first=False, last=False):
        start = at_least(line * 512 + pair * TILE, TILE)
        high, low = split(ug[pl.ds(start, TILE), :])
        uh[...] = high
        ul[...] = low

        def step(i, _):
            rows = pl.ds(at_least(i * TILE, TILE), TILE)
            dh, dl = dhi[rows, pl.ds(start, TILE)], dlo[rows, pl.ds(start, TILE)]
            total = dot(dh, uh[...]) + dot(dl, uh[...]) + dot(dh, ul[...])
            if not first:
                total = total + wacc[rows, :]
            if last:
                high, low = split(total)
                whi[rows, :] = high
                wlo[rows, :] = low
            else:
                wacc[rows, :] = total
            return 0

        lax.fori_loop(0, 4, step, 0)

    pg.spread(1)
    us.spread(1)
    pg.wait(1, 2, 3)
    pg.wait(2, 0, 1)
    hand(1, 0, 1, 2, 3)
    hand(2, 0, 1, 2, 3)
    hand(0, 0, 1)
    us.wait(1, 2, 3)
    us.wait(2, 0, 1)
    us.wait(3, 0, 1, 2, 3)
    weight(yh, 0, first=True)
    pg.spread(2)
    us.spread(2)
    pg.wait(3, 0, 1, 2, 3)
    hand(3, 0, 1, 2, 3)
    hand(0, 2)
    weight(yh, 1)
    pg.spread(3)
    us.spread(3)
    hand(0, 3)
    pg.relay(1, 0, 1)
    us.relay(1, 0, 1)
    pg.relay(1, 2)
    us.relay(1, 2)
    hand(4, 0, 1)
    pg.wait(5, 0, 1)
    hand(5, 0, 1, 2)
    pg.relay(1, 3)
    us.relay(1, 3)
    pg.wait(4, 2, 3)
    hand(4, 2, 3)
    hand(5, 3)
    us.wait(4, 2, 3)
    us.wait(5, 0, 1)
    weight(1 - yh, x // 2)
    for piece in (0, 2, 1, 3):
        pg.wait(6, piece)
        hand(6, piece)
    us.wait(6, 0, 1, 2, 3)
    weight(1 - yh, 1 - x // 2, last=True)
    for slot in range(8):
        ring, pair = pg.where(slot)
        for piece in range(PIECES):
            arrived(
                p_other(ring, pair, piece), core_recv.at[PIECES * slot + piece], send_sems.at[0], partner
            )

    def my_rows(i):
        return pl.ds(at_least(tile_of(i) * TILE + core * 128, 128), 128)

    def its_rows(i):
        return pl.ds(at_least(tile_of(i) * TILE + 128 - core * 128, 128), 128)

    def to_partner(i):
        return pltpu.make_async_remote_copy(
            src_ref=part.at[its_rows(i), :], dst_ref=rc.at[i], send_sem=rs_send.at[i], recv_sem=rc_recv.at[i],
            device_id=partner, device_id_type=MESH,
        )

    def far(i, half, way):
        return pltpu.make_async_remote_copy(
            src_ref=part.at[my_rows(i), pl.ds(way * 256, 256)], dst_ref=rz2.at[way, half],
            send_sem=rs_send.at[8 + 2 * way + half], recv_sem=rz2_recv.at[2 * way + half],
            device_id=z_minus if way else z_plus, device_id_type=MESH,
        )

    def near(i, half, way):
        return pltpu.make_async_remote_copy(
            src_ref=part.at[my_rows(i), :], dst_ref=rz.at[way, half],
            send_sem=rs_send.at[12 + 2 * way + half], recv_sem=rz_recv.at[2 * way + half],
            device_id=z_minus if way else z_plus, device_id_type=MESH,
        )

    def across():
        return pltpu.make_async_remote_copy(
            src_ref=part.at[my_rows(3), :], dst_ref=ry, send_sem=rs_send.at[16], recv_sem=ry_recv.at[0],
            device_id=y_pair, device_id_type=MESH,
        )

    def handle(i):
        half = i // 4
        j = i % 4
        mine = my_rows(i)
        to_partner(i).wait_recv()
        part[mine, :] = part[mine, :] + rc[i]

        @pl.when(j == 0)
        def _():
            far(i, half, 0).start()
            far(i, half, 1).start()

        for way in range(2):
            @pl.when(j == 1 + way)
            def _():
                far(i, half, way).wait_recv()
                lanes = pl.ds(way * 256, 256)
                part[mine, lanes] = part[mine, lanes] + rz2[way, half]
                near(i, half, way).start()

    def gather_line(i, half):
        mine = my_rows(i)
        near(i, half, 0).wait_recv()
        near(i, half, 1).wait_recv()
        part[mine, :] = part[mine, :] + rz[0, half] + rz[1, half]

    def prepare(i):
        rows = pl.ds(at_least(tile_of(i) * TILE, TILE), TILE)
        high, low = split(pt[:, rows].T)
        ph[i % 2] = high
        pl_[i % 2] = low

    prepare(0)

    def tile(i, _):
        m = tile_of(i)
        rows = pl.ds(at_least(m * TILE, TILE), TILE)
        front_copy(i).wait()

        @pl.when(i < 7)
        def _():
            front_copy(i + 1).start()

        high = ph[i % 2]
        update = dot(high, whi[...]) + dot(pl_[i % 2], whi[...]) + dot(high, wlo[...])
        s = fr[i % 2] - update
        schur[rows, :] = s
        prepare((i + 1) % 8)
        row_leaf = row * 16 + m * 2 + lax.broadcasted_iota(jnp.int32, (TILE, 1024), 0) // LEAF
        col_leaf = col * 8 + lax.broadcasted_iota(jnp.int32, (TILE, 1024), 1) // LEAF
        high, low = split(jnp.where(row_leaf == col_leaf, 0.0, s))

        @pl.when(i > 0)
        def _():
            handle(i - 1)

        @pl.when(i == 7)
        def _():
            gather_line(3, 0)
            across().start()

        part[rows, :] = dot(high, thi[...]) + dot(low, thi[...]) + dot(high, tlo[...])
        to_partner(i).start()
        return 0

    lax.fori_loop(0, 8, tile, 0)

    side = col % 2

    def leaf_block(k):
        return schur.at[pl.ds(at_least((side * 8 + k) * LEAF, LEAF), LEAF), pl.ds(k * LEAF, LEAF)]

    def leaf_copy(k):
        return pltpu.make_async_remote_copy(
            src_ref=leaf_block(k), dst_ref=leaf, send_sem=leaf_send.at[k], recv_sem=leaf_recv.at[0],
            device_id=(row, side * 8 + k), device_id_type=MESH,
        )

    for k in range(8):
        @pl.when((col // 2 == row) & (side * 8 + k != col))
        def _():
            leaf_copy(k).start()

        @pl.when((col // 2 == row) & (side * 8 + k == col))
        def _():
            pltpu.make_async_copy(leaf_block(k), leaf, local.at[4]).start()

    handle(7)
    gather_line(7, 1)
    across().wait_recv()
    mine = my_rows(7)
    samples = part[mine, :] + ry[...]
    off[...] = samples
    sends.start(off, sx, g_recv.at[0], partner)

    uh[:128, :512], ul[:128, :512] = split(samples)
    arrived(sx, g_recv.at[0], send_sems.at[0], partner)
    uh[128:, :512], ul[128:, :512] = split(sx[...])
    for t in range(5):
        i = (1 - core) * (t // 4) + core * (1 + t // 2)
        j = (1 - core) * (t % 4 + t // 4) + core * (2 + t % 2 + t // 4)
        left, right = pl.ds(at_least(i * 128, 128), 128), pl.ds(at_least(j * 128, 128), 128)
        gl[t * 128 : (t + 1) * 128, :] = (
            dot_tn(uh[:, left], uh[:, right]) + dot_tn(ul[:, left], uh[:, right]) + dot_tn(uh[:, left], ul[:, right])
        )

    def chip(q):
        yy, zz = plane(q)
        return yy * 4 + zz, (x * 2 + yy // 2, (yy % 2) * 8 + zz * 2 + core)

    def share(side, q):
        return gf.at[pl.ds(at_least(side * 640 + chip(q)[0] * 40, 8), 40), :]

    for q in range(1, 16):
        index, device = chip(q)
        sends.start(gl.at[pl.ds(at_least(index * 40, 8), 40), :], ga.at[q], g_recv.at[q], device)
    own = chip(0)[0]
    total = gl[pl.ds(at_least(own * 40, 8), 40), :]
    for q in range(1, 16):
        arrived(ga.at[q], g_recv.at[q], send_sems.at[0], partner)
        total = total + ga[q]
    gf[pl.ds(at_least(core * 640 + own * 40, 8), 40), :] = total * (1.0 / 4096)
    for q in range(1, 16):
        sends.start(share(core, 0), share(core, 0), g_recv.at[15 + q], chip(q)[1])
    sends.start(share(core, 0), share(core, 0), g_recv.at[31], partner)
    for q in range(1, 16):
        back = (4 - q // 4) % 4 * 4 + (4 - q % 4) % 4
        arrived(share(core, back), g_recv.at[15 + q], send_sems.at[0], partner)
        sends.start(share(core, back), share(core, back), g_recv.at[31 + q], partner)
    for q in range(16):
        back = (4 - q // 4) % 4 * 4 + (4 - q % 4) % 4
        arrived(share(1 - core, back), g_recv.at[31 + q], send_sems.at[0], partner)
    blocks = ((0, 0), (0, 1), (0, 2), (0, 3), (1, 1), (1, 2), (1, 3), (2, 2), (2, 3), (3, 3))
    for b, (i, j) in enumerate(blocks):
        block = gf[b * 128 : (b + 1) * 128, :]
        gram[i * 128 : (i + 1) * 128, j * 128 : (j + 1) * 128] = block
        if i != j:
            gram[j * 128 : (j + 1) * 128, i * 128 : (i + 1) * 128] = block.T

    holder = row * 2 + col // 8

    @pl.when(holder != col)
    def _():
        leaf_copy(0).wait_recv()

    @pl.when(holder == col)
    def _():
        pltpu.make_async_copy(leaf_block(0), leaf, local.at[4]).wait()

    for k in range(8):
        @pl.when((col // 2 == row) & (side * 8 + k != col))
        def _():
            leaf_copy(k).wait_send()

    for i in range(8):
        to_partner(i).wait_send()
    for half in range(2):
        for way in range(2):
            far(4 * half, half, way).wait_send()
            near(4 * half + 1 + way, half, way).wait_send()
    across().wait_send()
    sends.finish()


def emit(*refs):
    copies = [pltpu.make_async_copy(refs[i], refs[4 + i], refs[8].at[i]) for i in range(4)]
    for copy in copies:
        copy.start()
    for copy in copies:
        copy.wait()


def body(front_trailing, panel_columns, panel_rows, pivots, diag_inverse, test_matrix):
    hbm = pl.BlockSpec(memory_space=pltpu.HBM)
    vmem, dma = pltpu.VMEM, pltpu.SemaphoreType.DMA
    schur, off, leaf, gram = pl.pallas_call(
        kernel,
        out_shape=(
            pltpu.VMEM((2048, 1024), F32),
            pltpu.VMEM((128, 512), F32),
            pltpu.VMEM((128, 128), F32),
            pltpu.VMEM((512, 512), F32),
        ),
        in_specs=[hbm, hbm, hbm, pl.BlockSpec(memory_space=pltpu.VMEM), hbm, hbm],
        out_specs=(pl.BlockSpec(memory_space=pltpu.VMEM),) * 4,
        scratch_shapes=[
            vmem((1024, 2048), F32),
            vmem((1024, 1024), F32),
            vmem((1024, 1024), BF16),
            vmem((1024, 1024), BF16),
            vmem((1024, 1024), F32),
            vmem((1024, 1024), BF16),
            vmem((1024, 1024), BF16),
            vmem((TILE, 1024), BF16),
            vmem((TILE, 1024), BF16),
            vmem((2, TILE, 1024), BF16),
            vmem((2, TILE, 1024), BF16),
            vmem((2, TILE, 1024), F32),
            vmem((1024, 512), BF16),
            vmem((1024, 512), BF16),
            vmem((2048, 512), F32),
            vmem((8, 128, 512), F32),
            vmem((2, 2, 128, 256), F32),
            vmem((2, 2, 128, 512), F32),
            vmem((128, 512), F32),
            vmem((128, 512), F32),
            vmem((640, 128), F32),
            vmem((16, 40, 128), F32),
            vmem((1280, 128), F32),
            dma((160,)),
            dma((7 * PIECES,)),
            dma((8 * PIECES,)),
            dma((7 * PIECES,)),
            dma((17,)),
            dma((8,)),
            dma((4,)),
            dma((4,)),
            dma((1,)),
            dma((48,)),
            dma((8,)),
            dma((1,)),
            dma((5,)),
            dma((2,)),
        ],
        compiler_params=pltpu.CompilerParams(
            collective_id=0, has_side_effects=True, vmem_limit_bytes=49_000_000
        ),
        name="front",
    )(*[pltpu.with_memory_space_constraint(a, pltpu.HBM) for a in (front_trailing, panel_columns.T, panel_rows)],
      pivots.reshape(1, -1), *[pltpu.with_memory_space_constraint(a, pltpu.HBM) for a in (diag_inverse, test_matrix)])
    schur, off, leaf, gram = pl.pallas_call(
        emit,
        out_shape=[jax.ShapeDtypeStruct(a.shape, F32) for a in (schur, off, leaf, gram)],
        in_specs=[pl.BlockSpec(memory_space=pltpu.VMEM)] * 4,
        out_specs=[hbm] * 4,
        scratch_shapes=[dma((4,))],
        compiler_params=pltpu.CompilerParams(vmem_limit_bytes=2_000_000),
        name="emit",
    )(schur, off, leaf, gram)
    return schur, off, leaf, gram[None]


def solution(mesh):
    placed = (P("row", "col"), P("row", "col"), P("row", "col"), P(), P(), P("col", None))
    return jax.shard_map(
        body,
        mesh=mesh,
        in_specs=placed,
        out_specs=(
            P("row", "col"),
            P(("row", "col"), None),
            P(("row", "col"), None),
            P("row", None, None),
        ),
        check_vma=False,
    )
```

time: 121 us -> 105 us (0.87)
  local copies, waits for them, and re-layouts: 10.9 us -> 0 us
  Pallas kernels: 108 us -> 104 us
    unnamed x10 -> x0, local copies, waits for them, and re-layouts: 10.9 us -> none
    pallas_call x1 -> x2, Pallas kernels: 108 us -> 104 us  [the longest x1 100 us: body(): pl.pallas_call(kernel, out_shape=(pltpu.VMEM((2048, 1024), F32), pltpu.VM...]
where the time goes in v3:
time: 105 us
  Pallas kernels  104 us (99%)
    pallas_call x1, Pallas kernels, body(): pl.pallas_call(kernel, out_shape=(pltpu.VMEM((2048, 1024), F32), pltpu.VM...  100 us
    pallas_call x1, Pallas kernels, body(): pl.pallas_call(emit, out_shape=[jax.ShapeDtypeStruct(a.shape, F32) for a...  3.87 us

profile of v3, /device:TPU:0, one launch (start us, length us, event | category | flops | bytes accessed | tf_op | source)
XLA Modules:
  0.0 104.7 jit_solution(8745805283873350544)
XLA Ops:
  0.6 100.2 %front.1 = (f32[2048,1024]{1,0:T(8,128)S(1)}, f32[128,512]{1,0:T(8,128)S(1)}, f32[128,128]{1,0:T(8,128)S(1)}, f32[512,512]{1,0:T(8,128)S(1)}) custom-call(f32[2048,1024]{1,0:T(8,128)} %front_hbm.1, f32[64,2048]{1,0:T(8,128)} %bitcast.3, f32[128,1024]{1,0:T(8,128)} %u_hbm.1, s32[1,1024]{1,0:T(1,128)} %bitcast.4, f32[1024,1024]{1,0:T(8,128)} %diag_hbm.1, ...), custom_call_target="tpu_custom_call" | custom-call | tf_op jit(solution)/shard_map/front/pallas_call | solution.py:499
  100.9 3.9 %emit.1 = (f32[2048,1024]{1,0:T(8,128)}, f32[128,512]{1,0:T(8,128)}, f32[128,128]{1,0:T(8,128)}, f32[512,512]{1,0:T(8,128)}) custom-call(f32[2048,1024]{1,0:T(8,128)S(1)} %get-tuple-element.12.refs_0_, f32[128,512]{1,0:T(8,128)S(1)} %get-tuple-element.13.refs_1_, f32[128,128]{1,0:T(8,128)S(1)} %get-tuple-element.14.refs_2_, ...), custom_call_target="tpu_custom_call" | custom-call | tf_op jit(solution)/shard_map/emit/pallas_call | solution.py:554

commit v4 on v3

--- a/solution.py
+++ b/solution.py
@@ -36,26 +36,21 @@
 
 
 class Sends:
-    def __init__(self, sems):
-        self.sems, self.made = sems, []
+    def __init__(self, sem):
+        self.sem, self.count = sem, 0
 
     def start(self, src, dst, recv, device):
-        copy = pltpu.make_async_remote_copy(
-            src_ref=src, dst_ref=dst, send_sem=self.sems.at[len(self.made)], recv_sem=recv,
-            device_id=device, device_id_type=MESH,
-        )
-        copy.start()
-        self.made.append(copy)
-
-    def finish(self):
-        for copy in self.made:
-            copy.wait_send()
-
-
-def arrived(dst, recv, send, device):
-    pltpu.make_async_remote_copy(
-        src_ref=dst, dst_ref=dst, send_sem=send, recv_sem=recv, device_id=device, device_id_type=MESH
-    ).wait_recv()
+        self.count += 1
+        pltpu.make_async_remote_copy(
+            src_ref=src, dst_ref=dst, send_sem=self.sem, recv_sem=recv, device_id=device, device_id_type=MESH
+        ).start()
+
+    def finish(self, whole):
+        pltpu.make_async_copy(whole, whole, self.sem).wait()
+
+
+def arrived(dst, recv):
+    pltpu.make_async_copy(dst, dst, recv).wait()
 
 
 PIECES = 4
@@ -66,12 +61,13 @@
         self.sends, self.recv, self.source, self.place = sends, recv, source, place
         self.plus, self.minus, self.pair = plus, minus, pair
 
-    def begin(self):
-        for piece in range(PIECES):
-            src, dst = self.source(piece), self.place(0, 0, piece)
-            self.sends.start(src, dst, self.recv.at[piece], self.pair)
-            self.sends.start(src, dst, self.recv.at[PIECES + piece], self.plus)
-            self.sends.start(src, dst, self.recv.at[2 * PIECES + piece], self.minus)
+    def to_pair(self, piece):
+        self.sends.start(self.source(piece), self.place(0, 0, piece), self.recv.at[piece], self.pair)
+
+    def own(self, piece):
+        src, dst = self.source(piece), self.place(0, 0, piece)
+        self.sends.start(src, dst, self.recv.at[PIECES + piece], self.plus)
+        self.sends.start(src, dst, self.recv.at[2 * PIECES + piece], self.minus)
 
     def where(self, slot):
         return {0: 0, 1: -1, 2: 1, 3: 2, 4: -1, 5: 1, 6: 2, 7: 0}[slot], int(slot in (0, 4, 5, 6))
@@ -79,24 +75,20 @@
     def wait(self, slot, *pieces):
         ring, pair = self.where(slot)
         for piece in pieces:
-            arrived(
-                self.place(ring, pair, piece), self.recv.at[PIECES * slot + piece], self.sends.sems.at[0], self.plus
-            )
-
-    def spread(self, *pieces):
-        self.wait(0, *pieces)
-        for piece in pieces:
-            ref = self.place(0, 1, piece)
+            arrived(self.place(ring, pair, piece), self.recv.at[PIECES * slot + piece])
+
+    def spread(self, piece, up=True, down=True):
+        ref = self.place(0, 1, piece)
+        if up:
             self.sends.start(ref, ref, self.recv.at[4 * PIECES + piece], self.plus)
+        if down:
             self.sends.start(ref, ref, self.recv.at[5 * PIECES + piece], self.minus)
 
-    def relay(self, pair, *pieces):
-        slot = 6 if pair else 3
-        for piece in pieces:
-            ring, device = (-1, self.plus) if piece < 2 else (1, self.minus)
-            self.wait((1 if ring < 0 else 2) + 3 * pair, piece)
-            ref = self.place(ring, pair, piece)
-            self.sends.start(ref, ref, self.recv.at[PIECES * slot + piece], device)
+    def relay(self, pair, piece):
+        ring, device = (1, self.minus) if piece % 2 else (-1, self.plus)
+        self.wait((1 if ring < 0 else 2) + 3 * pair, piece)
+        ref = self.place(ring, pair, piece)
+        self.sends.start(ref, ref, self.recv.at[PIECES * (6 if pair else 3) + piece], device)
 
 
 def kernel(
@@ -146,34 +138,36 @@
         pl.semaphore_signal(barrier, inc=1, device_id=peer, device_id_type=MESH)
     pl.semaphore_wait(barrier, len(peers))
 
-    sends = Sends(send_sems)
+    p_sends, u_sends = Sends(send_sems.at[0]), Sends(send_sems.at[1])
 
     def p_place(dz, dy, piece):
         return pt.at[pl.ds(at_least(p_col(dz, dy) * 64, 64), 64), pl.ds(piece * 512, 512)]
 
-    def p_other(dz, dy, piece):
-        c = p_col(dz, dy) + 1 - 2 * core
-        return pt.at[pl.ds(at_least(c * 64, 64), 64), pl.ds(piece * 512, 512)]
-
     def u_place(dx, dy, piece):
-        return ug.at[pl.ds(at_least(((yh + dy) % 2) * 512 + ((x + dx + 4) % 4) * 128 + piece * 32, 32), 32), :]
-
-    pg = Gather(sends, p_recv, lambda i: pt_hbm.at[:, pl.ds(i * 512, 512)], p_place, z_plus, z_minus, y_pair)
-    us = Gather(sends, u_recv, lambda i: u_hbm.at[pl.ds(i * 32, 32), :], u_place, x_plus, x_minus, h_pair)
-    pg.begin()
-    us.begin()
+        rows = pl.ds(at_least(((yh + dy) % 2) * 512 + ((x + dx + 4) % 4) * 128, 128), 128)
+        return ug.at[rows, pl.ds(piece * 256, 256)]
+
+    pg = Gather(p_sends, p_recv, lambda i: pt_hbm.at[:, pl.ds(i * 512, 512)], p_place, z_plus, z_minus, y_pair)
+    us = Gather(u_sends, u_recv, lambda i: u_hbm.at[:, pl.ds(i * 256, 256)], u_place, x_plus, x_minus, h_pair)
+    both = (pg, us)
     for piece in range(PIECES):
-        sends.start(pg.source(piece), p_place(0, 0, piece), core_recv.at[7 * PIECES + piece], partner)
+        for g in both:
+            g.to_pair(piece)
+    for piece in range(2):
+        for g in both:
+            g.own(piece)
+    for piece in range(PIECES):
+        p_sends.start(pg.source(piece), p_place(0, 0, piece), core_recv.at[piece // 2], partner)
 
     def hand(slot, *pieces):
         ring, pair = pg.where(slot)
         for piece in pieces:
             ref = p_place(ring, pair, piece)
-            sends.start(ref, ref, core_recv.at[PIECES * slot + piece], partner)
+            p_sends.start(ref, ref, core_recv.at[piece // 2], partner)
 
     def tile_of(i):
-        half = i // 4
-        j = i % 4
+        half = i % 2
+        j = i // 2
         off = 2 - j + 3 * (j // 2) - 2 * (j // 3)
         return ((yl + 1 - half) % 2) * 4 + (z + off) % 4
 
@@ -181,7 +175,14 @@
         rows = pl.ds(at_least(tile_of(i) * TILE, TILE), TILE)
         return pltpu.make_async_copy(front_hbm.at[rows, :], fr.at[i % 2], front_sem.at[i % 2])
 
-    front_copy(0).start()
+    def early_front(m):
+        lanes = pl.ds(0, 512)
+        return pltpu.make_async_copy(
+            front_hbm.at[pl.ds(m * TILE, TILE), lanes], fr.at[m % 2, :, lanes], front_sem.at[m % 2]
+        )
+
+    early_front(0).start()
+    early_front(1).start()
 
     def one_hot(i, _):
         rows = pl.ds(at_least(i * TILE, TILE), TILE)
@@ -200,14 +201,15 @@
         dlo[rows, :] = dot_nt(low, whi[...]).astype(BF16)
         return 0
 
-    lax.fori_loop(0, 3, permute, 0)
-    pg.relay(0, 0, 1, 2)
-    us.relay(0, 0, 1, 2)
-    lax.fori_loop(3, 4, permute, 0)
-    pg.relay(0, 3)
-    us.relay(0, 3)
-    pg.spread(0)
-    us.spread(0)
+    lax.fori_loop(0, 2, permute, 0)
+    for g in both:
+        g.relay(0, 0)
+        g.relay(0, 1)
+    for g in both:
+        g.wait(0, 0)
+        g.spread(0)
+        g.own(2)
+    lax.fori_loop(2, 4, permute, 0)
     for copy in loads[1:]:
         copy.wait()
 
@@ -220,74 +222,135 @@
 
     lax.fori_loop(0, 4, split_test, 0)
 
-    def weight(line, pair, first=False, last=False):
+    def weight(line, pair, half, first=False, last=False):
         start = at_least(line * 512 + pair * TILE, TILE)
-        high, low = split(ug[pl.ds(start, TILE), :])
-        uh[...] = high
-        ul[...] = low
+        lanes = slice(half * 512, half * 512 + 512)
+        uh[:, :512], ul[:, :512] = split(ug[pl.ds(start, TILE), lanes])
 
         def step(i, _):
             rows = pl.ds(at_least(i * TILE, TILE), TILE)
             dh, dl = dhi[rows, pl.ds(start, TILE)], dlo[rows, pl.ds(start, TILE)]
-            total = dot(dh, uh[...]) + dot(dl, uh[...]) + dot(dh, ul[...])
+            total = dot(dh, uh[:, :512]) + dot(dl, uh[:, :512]) + dot(dh, ul[:, :512])
             if not first:
-                total = total + wacc[rows, :]
+                total = total + wacc[rows, lanes]
             if last:
-                high, low = split(total)
-                whi[rows, :] = high
-                wlo[rows, :] = low
+                whi[rows, lanes], wlo[rows, lanes] = split(total)
             else:
-                wacc[rows, :] = total
+                wacc[rows, lanes] = total
             return 0
 
         lax.fori_loop(0, 4, step, 0)
 
-    pg.spread(1)
-    us.spread(1)
-    pg.wait(1, 2, 3)
-    pg.wait(2, 0, 1)
-    hand(1, 0, 1, 2, 3)
-    hand(2, 0, 1, 2, 3)
-    hand(0, 0, 1)
-    us.wait(1, 2, 3)
-    us.wait(2, 0, 1)
-    us.wait(3, 0, 1, 2, 3)
-    weight(yh, 0, first=True)
-    pg.spread(2)
-    us.spread(2)
-    pg.wait(3, 0, 1, 2, 3)
-    hand(3, 0, 1, 2, 3)
+    def from_partner(which):
+        arrived(pt.at[pl.ds(0, 256), :], core_recv.at[which])
+
+    def prepare(m, slot):
+        rows = pl.ds(at_least(m * TILE, TILE), TILE)
+        ph[slot], pl_[slot] = split(pt[:, rows].T)
+
+    def half_tile(m, slot, half, ahead=None, between=None):
+        rows = pl.ds(at_least(m * TILE, TILE), TILE)
+        lanes = slice(half * 512, half * 512 + 512)
+        high = ph[slot]
+        update = dot(high, whi[:, lanes]) + dot(pl_[slot], whi[:, lanes]) + dot(high, wlo[:, lanes])
+        if ahead is not None:
+            ahead()
+        s = fr[slot, :, lanes] - update
+        schur[rows, lanes] = s
+        row_leaf = row * 16 + m * 2 + lax.broadcasted_iota(jnp.int32, (TILE, 512), 0) // LEAF
+        col_leaf = col * 8 + half * 4 + lax.broadcasted_iota(jnp.int32, (TILE, 512), 1) // LEAF
+        high, low = split(jnp.where(row_leaf == col_leaf, 0.0, s))
+        if between is not None:
+            between()
+        samples = dot(high, thi[lanes, :]) + dot(low, thi[lanes, :]) + dot(high, tlo[lanes, :])
+        part[rows, :] = part[rows, :] + samples if half else samples
+
+    def early(m):
+        early_front(m).wait()
+        if m == 0:
+            prepare(0, 0)
+        half_tile(m, m % 2, 0, None if m == 3 else lambda: prepare(m + 1, (m + 1) % 2))
+        if m < 2:
+            early_front(m + 2).start()
+
+    pg.wait(1, 1)
+    pg.wait(2, 0)
+    hand(1, 0, 1)
+    hand(2, 0, 1)
+    hand(0, 0)
+    us.wait(1, 1)
+    us.wait(2, 0)
+    pg.wait(3, 0, 1)
+    hand(3, 0, 1)
+    us.wait(3, 0, 1)
+    for g in both:
+        g.wait(0, 1)
+        g.spread(1)
+    hand(0, 1)
+    weight(yh, 0, 0, first=True)
+    for g in both:
+        g.relay(1, 0)
+        g.own(3)
+    hand(4, 0)
+    weight(yh, 1, 0)
+    for g in both:
+        g.relay(1, 1)
+        g.relay(0, 2)
+        g.wait(0, 2)
+        g.spread(2)
+    pg.wait(5, 0)
+    pg.wait(4, 1)
+    hand(5, 0, 1)
+    hand(4, 1)
+    us.wait(5, 0)
+    us.wait(4, 1)
+    weight(1 - yh, x // 2, 0)
+    for g in both:
+        g.relay(0, 3)
     hand(0, 2)
-    weight(yh, 1)
-    pg.spread(3)
-    us.spread(3)
+    pg.wait(6, 0, 1)
+    hand(6, 0, 1)
+    us.wait(6, 0, 1)
+    weight(1 - yh, 1 - x // 2, 0, last=True)
+    from_partner(0)
+    early(0)
+    for g in both:
+        g.wait(0, 3)
+        g.spread(3)
     hand(0, 3)
-    pg.relay(1, 0, 1)
-    us.relay(1, 0, 1)
-    pg.relay(1, 2)
-    us.relay(1, 2)
-    hand(4, 0, 1)
-    pg.wait(5, 0, 1)
-    hand(5, 0, 1, 2)
-    pg.relay(1, 3)
-    us.relay(1, 3)
-    pg.wait(4, 2, 3)
-    hand(4, 2, 3)
+    pg.wait(1, 3)
+    pg.wait(2, 2)
+    hand(1, 2, 3)
+    hand(2, 2, 3)
+    us.wait(1, 3)
+    us.wait(2, 2)
+    early(1)
+    for g in both:
+        g.relay(1, 2)
+    hand(4, 2)
+    pg.wait(3, 2, 3)
+    hand(3, 2, 3)
+    us.wait(3, 2, 3)
+    early(2)
+    weight(yh, 0, 1, first=True)
+    for g in both:
+        g.relay(1, 3)
     hand(5, 3)
-    us.wait(4, 2, 3)
-    us.wait(5, 0, 1)
-    weight(1 - yh, x // 2)
-    for piece in (0, 2, 1, 3):
-        pg.wait(6, piece)
-        hand(6, piece)
-    us.wait(6, 0, 1, 2, 3)
-    weight(1 - yh, 1 - x // 2, last=True)
-    for slot in range(8):
-        ring, pair = pg.where(slot)
-        for piece in range(PIECES):
-            arrived(
-                p_other(ring, pair, piece), core_recv.at[PIECES * slot + piece], send_sems.at[0], partner
-            )
+    early(3)
+    front_copy(0).start()
+    weight(yh, 1, 1)
+    pg.wait(4, 3)
+    pg.wait(5, 2)
+    hand(4, 3)
+    hand(5, 2)
+    us.wait(4, 3)
+    us.wait(5, 2)
+    weight(1 - yh, x // 2, 1)
+    pg.wait(6, 2, 3)
+    hand(6, 2, 3)
+    us.wait(6, 2, 3)
+    weight(1 - yh, 1 - x // 2, 1, last=True)
+    from_partner(1)
 
     def my_rows(i):
         return pl.ds(at_least(tile_of(i) * TILE + core * 128, 128), 128)
@@ -317,13 +380,13 @@
 
     def across():
         return pltpu.make_async_remote_copy(
-            src_ref=part.at[my_rows(3), :], dst_ref=ry, send_sem=rs_send.at[16], recv_sem=ry_recv.at[0],
+            src_ref=part.at[my_rows(6), :], dst_ref=ry, send_sem=rs_send.at[16], recv_sem=ry_recv.at[0],
             device_id=y_pair, device_id_type=MESH,
         )
 
     def handle(i):
-        half = i // 4
-        j = i % 4
+        half = i % 2
+        j = i // 2
         mine = my_rows(i)
         to_partner(i).wait_recv()
         part[mine, :] = part[mine, :] + rc[i]
@@ -347,42 +410,35 @@
         near(i, half, 1).wait_recv()
         part[mine, :] = part[mine, :] + rz[0, half] + rz[1, half]
 
-    def prepare(i):
-        rows = pl.ds(at_least(tile_of(i) * TILE, TILE), TILE)
-        high, low = split(pt[:, rows].T)
-        ph[i % 2] = high
-        pl_[i % 2] = low
-
-    prepare(0)
+    prepare(tile_of(0), 0)
 
     def tile(i, _):
         m = tile_of(i)
-        rows = pl.ds(at_least(m * TILE, TILE), TILE)
+        slot = i % 2
         front_copy(i).wait()
 
         @pl.when(i < 7)
         def _():
             front_copy(i + 1).start()
 
-        high = ph[i % 2]
-        update = dot(high, whi[...]) + dot(pl_[i % 2], whi[...]) + dot(high, wlo[...])
-        s = fr[i % 2] - update
-        schur[rows, :] = s
-        prepare((i + 1) % 8)
-        row_leaf = row * 16 + m * 2 + lax.broadcasted_iota(jnp.int32, (TILE, 1024), 0) // LEAF
-        col_leaf = col * 8 + lax.broadcasted_iota(jnp.int32, (TILE, 1024), 1) // LEAF
-        high, low = split(jnp.where(row_leaf == col_leaf, 0.0, s))
-
-        @pl.when(i > 0)
+        @pl.when(m >= 4)
         def _():
-            handle(i - 1)
-
-        @pl.when(i == 7)
-        def _():
-            gather_line(3, 0)
-            across().start()
-
-        part[rows, :] = dot(high, thi[...]) + dot(low, thi[...]) + dot(high, tlo[...])
+            half_tile(m, slot, 0)
+
+        def ahead():
+            prepare(tile_of((i + 1) % 8), (i + 1) % 2)
+
+        def between():
+            @pl.when(i > 0)
+            def _():
+                handle(i - 1)
+
+            @pl.when(i == 7)
+            def _():
+                gather_line(6, 0)
+                across().start()
+
+        half_tile(m, slot, 1, ahead, between)
         to_partner(i).start()
         return 0
 
@@ -414,10 +470,11 @@
     mine = my_rows(7)
     samples = part[mine, :] + ry[...]
     off[...] = samples
-    sends.start(off, sx, g_recv.at[0], partner)
+    x_sends, s_sends, t_sends, f_sends = (Sends(send_sems.at[2 + i]) for i in range(4))
+    x_sends.start(off, sx, g_recv.at[0], partner)
 
     uh[:128, :512], ul[:128, :512] = split(samples)
-    arrived(sx, g_recv.at[0], send_sems.at[0], partner)
+    arrived(sx, g_recv.at[0])
     uh[128:, :512], ul[128:, :512] = split(sx[...])
     for t in range(5):
         i = (1 - core) * (t // 4) + core * (1 + t // 2)
@@ -436,23 +493,21 @@
 
     for q in range(1, 16):
         index, device = chip(q)
-        sends.start(gl.at[pl.ds(at_least(index * 40, 8), 40), :], ga.at[q], g_recv.at[q], device)
+        s_sends.start(gl.at[pl.ds(at_least(index * 40, 8), 40), :], ga.at[q], g_recv.at[1], device)
     own = chip(0)[0]
     total = gl[pl.ds(at_least(own * 40, 8), 40), :]
+    arrived(ga.at[pl.ds(1, 15)], g_recv.at[1])
     for q in range(1, 16):
-        arrived(ga.at[q], g_recv.at[q], send_sems.at[0], partner)
         total = total + ga[q]
     gf[pl.ds(at_least(core * 640 + own * 40, 8), 40), :] = total * (1.0 / 4096)
     for q in range(1, 16):
-        sends.start(share(core, 0), share(core, 0), g_recv.at[15 + q], chip(q)[1])
-    sends.start(share(core, 0), share(core, 0), g_recv.at[31], partner)
+        t_sends.start(share(core, 0), share(core, 0), g_recv.at[2 + q], chip(q)[1])
+    f_sends.start(share(core, 0), share(core, 0), g_recv.at[2], partner)
     for q in range(1, 16):
         back = (4 - q // 4) % 4 * 4 + (4 - q % 4) % 4
-        arrived(share(core, back), g_recv.at[15 + q], send_sems.at[0], partner)
-        sends.start(share(core, back), share(core, back), g_recv.at[31 + q], partner)
-    for q in range(16):
-        back = (4 - q // 4) % 4 * 4 + (4 - q % 4) % 4
-        arrived(share(1 - core, back), g_recv.at[31 + q], send_sems.at[0], partner)
+        arrived(share(core, back), g_recv.at[2 + q])
+        f_sends.start(share(core, back), share(core, back), g_recv.at[2], partner)
+    arrived(ga, g_recv.at[2])
     blocks = ((0, 0), (0, 1), (0, 2), (0, 3), (1, 1), (1, 2), (1, 3), (2, 2), (2, 3), (3, 3))
     for b, (i, j) in enumerate(blocks):
         block = gf[b * 128 : (b + 1) * 128, :]
@@ -479,10 +534,16 @@
         to_partner(i).wait_send()
     for half in range(2):
         for way in range(2):
-            far(4 * half, half, way).wait_send()
-            near(4 * half + 1 + way, half, way).wait_send()
+            far(half, half, way).wait_send()
+            near(2 + 2 * way + half, half, way).wait_send()
     across().wait_send()
-    sends.finish()
+    assert (p_sends.count, u_sends.count) == (60, 28)
+    p_sends.finish(pt.at[pl.ds(0, 960), :])
+    u_sends.finish(ug.at[pl.ds(0, 896), :])
+    x_sends.finish(off)
+    s_sends.finish(ga.at[pl.ds(1, 15)])
+    t_sends.finish(ga.at[pl.ds(1, 15)])
+    f_sends.finish(ga)
 
 
 def emit(*refs):
@@ -530,16 +591,16 @@
             vmem((640, 128), F32),
             vmem((16, 40, 128), F32),
             vmem((1280, 128), F32),
-            dma((160,)),
+            dma((6,)),
             dma((7 * PIECES,)),
-            dma((8 * PIECES,)),
+            dma((2,)),
             dma((7 * PIECES,)),
             dma((17,)),
             dma((8,)),
             dma((4,)),
             dma((4,)),
             dma((1,)),
-            dma((48,)),
+            dma((18,)),
             dma((8,)),
             dma((1,)),
             dma((5,)),

time: 105 us -> 104 us (level); the launches traced: 105 us -> 102 us
  Pallas kernels: 104 us -> 101 us
    pallas_call x1, Pallas kernels: 100 us -> 97.6 us  [body(): pl.pallas_call(kernel, out_shape=(pltpu.VMEM((2048, 1024), F32), pltpu.VM...]
where the time goes in v4:
time: 104 us; the launch traced here: 102 us
  Pallas kernels  101 us (97%)
    pallas_call x1, Pallas kernels, body(): pl.pallas_call(kernel, out_shape=(pltpu.VMEM((2048, 1024), F32), pltpu.VM...  97.6 us
    pallas_call x1, Pallas kernels, body(): pl.pallas_call(emit, out_shape=[jax.ShapeDtypeStruct(a.shape, F32) for a...  3.87 us

profile of v4, /device:TPU:0, one launch (start us, length us, event | category | flops | bytes accessed | tf_op | source)
XLA Modules:
  0.0 102.2 jit_solution(14723096008104679500)
XLA Ops:
  0.6 97.6 %front.1 = (f32[2048,1024]{1,0:T(8,128)S(1)}, f32[128,512]{1,0:T(8,128)S(1)}, f32[128,128]{1,0:T(8,128)S(1)}, f32[512,512]{1,0:T(8,128)S(1)}) custom-call(f32[2048,1024]{1,0:T(8,128)} %front_hbm.1, f32[64,2048]{1,0:T(8,128)} %bitcast.3, f32[128,1024]{1,0:T(8,128)} %u_hbm.1, s32[1,1024]{1,0:T(1,128)} %bitcast.4, f32[1024,1024]{1,0:T(8,128)} %diag_hbm.1, ...), custom_call_target="tpu_custom_call" | custom-call | tf_op jit(solution)/shard_map/front/pallas_call | solution.py:560
  98.2 3.9 %emit.1 = (f32[2048,1024]{1,0:T(8,128)}, f32[128,512]{1,0:T(8,128)}, f32[128,128]{1,0:T(8,128)}, f32[512,512]{1,0:T(8,128)}) custom-call(f32[2048,1024]{1,0:T(8,128)S(1)} %get-tuple-element.12.refs_0_, f32[128,512]{1,0:T(8,128)S(1)} %get-tuple-element.13.refs_1_, f32[128,128]{1,0:T(8,128)S(1)} %get-tuple-element.14.refs_2_, ...), custom_call_target="tpu_custom_call" | custom-call | tf_op jit(solution)/shard_map/emit/pallas_call | solution.py:615

commit v5 on v4

--- a/solution.py
+++ b/solution.py
@@ -239,7 +239,7 @@
                 wacc[rows, lanes] = total
             return 0
 
-        lax.fori_loop(0, 4, step, 0)
+        lax.fori_loop(0, 4, step, 0, unroll=True)
 
     def from_partner(which):
         arrived(pt.at[pl.ds(0, 256), :], core_recv.at[which])
@@ -546,8 +546,10 @@
     f_sends.finish(ga)
 
 
-def emit(*refs):
-    copies = [pltpu.make_async_copy(refs[i], refs[4 + i], refs[8].at[i]) for i in range(4)]
+def emit(schur, off, leaf, gram, schur_out, off_out, leaf_out, gram_out, sems):
+    pairs = [(schur.at[pl.ds(i * 512, 512), :], schur_out.at[pl.ds(i * 512, 512), :]) for i in range(4)]
+    pairs += [(gram, gram_out), (off, off_out), (leaf, leaf_out)]
+    copies = [pltpu.make_async_copy(src, dst, sems.at[i]) for i, (src, dst) in enumerate(pairs)]
     for copy in copies:
         copy.start()
     for copy in copies:
@@ -617,7 +619,7 @@
         out_shape=[jax.ShapeDtypeStruct(a.shape, F32) for a in (schur, off, leaf, gram)],
         in_specs=[pl.BlockSpec(memory_space=pltpu.VMEM)] * 4,
         out_specs=[hbm] * 4,
-        scratch_shapes=[dma((4,))],
+        scratch_shapes=[dma((7,))],
         compiler_params=pltpu.CompilerParams(vmem_limit_bytes=2_000_000),
         name="emit",
     )(schur, off, leaf, gram)

time: 104 us -> 103 us (level)
  no operation moved by 1% of the time
where the time goes in v5:
time: 103 us; the launch traced here: 102 us
  Pallas kernels  101 us (98%)
    pallas_call x1, Pallas kernels, body(): pl.pallas_call(kernel, out_shape=(pltpu.VMEM((2048, 1024), F32), pltpu.VM...  97.2 us
    pallas_call x1, Pallas kernels, body(): pl.pallas_call(emit, out_shape=[jax.ShapeDtypeStruct(a.shape, F32) for a...  3.73 us

profile of v5, /device:TPU:0, one launch (start us, length us, event | category | flops | bytes accessed | tf_op | source)
XLA Modules:
  0.0 101.7 jit_solution(8084111183568198268)
XLA Ops:
  0.6 97.2 %front.1 = (f32[2048,1024]{1,0:T(8,128)S(1)}, f32[128,512]{1,0:T(8,128)S(1)}, f32[128,128]{1,0:T(8,128)S(1)}, f32[512,512]{1,0:T(8,128)S(1)}) custom-call(f32[2048,1024]{1,0:T(8,128)} %front_hbm.1, f32[64,2048]{1,0:T(8,128)} %bitcast.3, f32[128,1024]{1,0:T(8,128)} %u_hbm.1, s32[1,1024]{1,0:T(1,128)} %bitcast.4, f32[1024,1024]{1,0:T(8,128)} %diag_hbm.1, ...), custom_call_target="tpu_custom_call" | custom-call | tf_op jit(solution)/shard_map/front/pallas_call | solution.py:562
  97.8 3.7 %emit.1 = (f32[2048,1024]{1,0:T(8,128)}, f32[128,512]{1,0:T(8,128)}, f32[128,128]{1,0:T(8,128)}, f32[512,512]{1,0:T(8,128)}) custom-call(f32[2048,1024]{1,0:T(8,128)S(1)} %get-tuple-element.12.schur, f32[128,512]{1,0:T(8,128)S(1)} %get-tuple-element.13.off, f32[128,128]{1,0:T(8,128)S(1)} %get-tuple-element.14.leaf, f32[512,512]{1,0:T(8,128)S(1)} %get-tuple-element.15.gram), custom_call_target="tpu_custom_call" | custom-call | tf_op jit(solution)/shard_map/emit/pallas_call | solution.py:617

commit v6 on v5

--- a/solution.py
+++ b/solution.py
@@ -206,9 +206,10 @@
         g.relay(0, 0)
         g.relay(0, 1)
     for g in both:
+        g.own(2)
+    for g in both:
         g.wait(0, 0)
         g.spread(0)
-        g.own(2)
     lax.fori_loop(2, 4, permute, 0)
     for copy in loads[1:]:
         copy.wait()
@@ -286,11 +287,11 @@
     for g in both:
         g.wait(0, 1)
         g.spread(1)
+        g.own(3)
     hand(0, 1)
     weight(yh, 0, 0, first=True)
     for g in both:
         g.relay(1, 0)
-        g.own(3)
     hand(4, 0)
     weight(yh, 1, 0)
     for g in both:
@@ -360,7 +361,7 @@
 
     def to_partner(i):
         return pltpu.make_async_remote_copy(
-            src_ref=part.at[its_rows(i), :], dst_ref=rc.at[i], send_sem=rs_send.at[i], recv_sem=rc_recv.at[i],
+            src_ref=part.at[its_rows(i), :], dst_ref=rc.at[i], send_sem=rs_send.at[0], recv_sem=rc_recv.at[i],
             device_id=partner, device_id_type=MESH,
         )
 
@@ -530,8 +531,7 @@
         def _():
             leaf_copy(k).wait_send()
 
-    for i in range(8):
-        to_partner(i).wait_send()
+    pltpu.make_async_copy(rc, rc, rs_send.at[0]).wait()
     for half in range(2):
         for way in range(2):
             far(half, half, way).wait_send()

time: 103 us -> 103 us (level)
  no operation moved by 1% of the time
where the time goes in v6:
time: 103 us; the launch traced here: 102 us
  Pallas kernels  101 us (98%)
    pallas_call x1, Pallas kernels, body(): pl.pallas_call(kernel, out_shape=(pltpu.VMEM((2048, 1024), F32), pltpu.VM...  97.1 us
    pallas_call x1, Pallas kernels, body(): pl.pallas_call(emit, out_shape=[jax.ShapeDtypeStruct(a.shape, F32) for a...  3.73 us

profile of v6, /device:TPU:0, one launch (start us, length us, event | category | flops | bytes accessed | tf_op | source)
XLA Modules:
  0.0 101.7 jit_solution(957955477570098577)
XLA Ops:
  0.6 97.1 %front.1 = (f32[2048,1024]{1,0:T(8,128)S(1)}, f32[128,512]{1,0:T(8,128)S(1)}, f32[128,128]{1,0:T(8,128)S(1)}, f32[512,512]{1,0:T(8,128)S(1)}) custom-call(f32[2048,1024]{1,0:T(8,128)} %front_hbm.1, f32[64,2048]{1,0:T(8,128)} %bitcast.3, f32[128,1024]{1,0:T(8,128)} %u_hbm.1, s32[1,1024]{1,0:T(1,128)} %bitcast.4, f32[1024,1024]{1,0:T(8,128)} %diag_hbm.1, ...), custom_call_target="tpu_custom_call" | custom-call | tf_op jit(solution)/shard_map/front/pallas_call | solution.py:562
  97.8 3.7 %emit.1 = (f32[2048,1024]{1,0:T(8,128)}, f32[128,512]{1,0:T(8,128)}, f32[128,128]{1,0:T(8,128)}, f32[512,512]{1,0:T(8,128)}) custom-call(f32[2048,1024]{1,0:T(8,128)S(1)} %get-tuple-element.12.schur, f32[128,512]{1,0:T(8,128)S(1)} %get-tuple-element.13.off, f32[128,128]{1,0:T(8,128)S(1)} %get-tuple-element.14.leaf, f32[512,512]{1,0:T(8,128)S(1)} %get-tuple-element.15.gram), custom_call_target="tpu_custom_call" | custom-call | tf_op jit(solution)/shard_map/emit/pallas_call | solution.py:617
